TPU v7x, 512 devices: a whole 4x4x16 slice. The times are simulated.
512 devices in a mesh: state: 128 (over x, z, core), rep: 4 (over y).
Axes of the slice: x: 4, y: 4, z: 16, core: 2. Of those that a mesh axis runs over, the one named last changes fastest.
Arguments:
- ensemble: float32 [64, 524288], P('rep', 'state'), may hold values from -6 to 6
- obs_values: float32 [48], replicated, may hold values from -8 to 8
- obs_error: float32 [48], replicated, may hold values from 0.25 to 2
- obs_location: int32 [48], replicated, may hold values from 0 to 524287
Outputs:
- analysis: float32 [64, 524288], P('rep', 'state')
All inputs are finite; a program needn't handle non-finite values.
Results may differ from a plain program's by a relative error of at most 0.0001.
Values sent between devices are 32-bit elements; how exact they have to be, the bound alone decides.
A program may use at most 64 MiB of HBM per device.

v0:
```python
import jax
import jax.numpy as jnp
from jax import lax
from jax.sharding import PartitionSpec as P

M = 64
TILE = 128
SBLK = 8
BLOCKS = 3
BATCHES = 2
HALF = 4096


def taper(distance):
    ratio = distance / HALF
    near_part = (((-0.25 * ratio + 0.5) * ratio + 0.625) * ratio - 5.0 / 3.0) * ratio * ratio + 1.0
    ratio_far = jnp.maximum(ratio, 1.0)
    far_part = (
        ((((ratio_far / 12.0 - 0.5) * ratio_far + 0.625) * ratio_far + 5.0 / 3.0) * ratio_far - 5.0)
        * ratio_far
        + 4.0
        - 2.0 / (3.0 * ratio_far)
    )
    return jnp.where(
        ratio <= 1.0, near_part, jnp.where(ratio < 2.0, far_part, jnp.zeros_like(ratio))
    )


def centers_of(columns):
    return (columns // TILE * TILE).astype(jnp.float32) + (TILE - 1) * 0.5


def weights_of(column_centers, locations):
    return taper(jnp.abs(column_centers[None, :] - locations.astype(jnp.float32)[:, None]))


def block_factors(current_rows, values, errors, self_weights):
    u_list = []
    w_list = []
    for slot in range(current_rows.shape[1]):
        prior_col = current_rows[:, slot]
        mean_value = jnp.mean(prior_col)
        spread = prior_col - mean_value
        variance = jnp.sum(spread * spread) / (M - 1)
        total_var = variance + errors[slot]
        shrink = 1.0 / (1.0 + jnp.sqrt(errors[slot] / total_var))
        u_vec = spread / ((M - 1) * total_var)
        w_vec = values[slot] - mean_value - shrink * spread
        coefficient = self_weights[slot] * jnp.dot(
            u_vec, current_rows, precision=lax.Precision.HIGHEST
        )
        current_rows = current_rows + w_vec[:, None] * coefficient[None, :]
        u_list.append(u_vec)
        w_list.append(w_vec)
    return (jnp.stack(u_list, axis=1), jnp.stack(w_list, axis=1))


def solve_scaled(projected, weights, mixing):
    scaled = []
    for slot in range(projected.shape[0]):
        running = projected[slot]
        if slot > 0:
            running = running + jnp.dot(
                mixing[:slot, slot], jnp.stack(scaled), precision=lax.Precision.HIGHEST
            )
        scaled.append(weights[slot] * running)
    return jnp.stack(scaled)


def picked(current, chosen, column_start, rep_index):
    columns_held = current.shape[1]
    offsets = chosen - column_start
    inside = ((offsets >= 0) & (offsets < columns_held)).astype(jnp.float32)
    selected = jnp.take(current, jnp.clip(offsets, 0, columns_held - 1), axis=1) * inside[None, :]
    placed = jnp.zeros((M, chosen.shape[0]), jnp.float32)
    return lax.dynamic_update_slice(placed, selected, (rep_index * current.shape[0], 0))


def on_device(ensemble, obs_values, obs_error, obs_location):
    rep_index = lax.axis_index("rep")
    state_index = lax.axis_index("state")
    held_count = ensemble.shape[1]
    part_rows = ensemble.shape[0]
    current = ensemble
    column_start = state_index * held_count
    columns_held = current.shape[1]
    column_centers = centers_of(column_start + lax.iota(jnp.int32, columns_held))
    batch_width = BLOCKS * SBLK
    for batch_index in range(BATCHES):
        batch_start = batch_index * batch_width
        for block_index in range(BLOCKS):
            block_start = batch_start + block_index * SBLK
            block_locs = obs_location[block_start : block_start + SBLK]
            values = obs_values[block_start : block_start + SBLK]
            errors = obs_error[block_start : block_start + SBLK]
            current_rows = lax.psum(
                picked(current, block_locs, column_start, rep_index), ("state", "rep")
            )
            self_weights = weights_of(centers_of(block_locs), block_locs)
            u_factors, w_factors = block_factors(current_rows, values, errors, self_weights)
            mixing = jnp.dot(w_factors.T, u_factors, precision=lax.Precision.HIGHEST)
            u_local = lax.dynamic_slice_in_dim(u_factors, rep_index * part_rows, part_rows, 0)
            w_local = lax.dynamic_slice_in_dim(w_factors, rep_index * part_rows, part_rows, 0)
            partial_value = jnp.dot(u_local.T, current, precision=lax.Precision.HIGHEST)
            projected = lax.psum(partial_value, "rep")
            weights = weights_of(column_centers, block_locs)
            scaled = solve_scaled(projected, weights, mixing)
            current = current + jnp.dot(w_local, scaled, precision=lax.Precision.HIGHEST)
    return current


def solution(mesh):
    in_specs = (P("rep", "state"), P(), P(), P())
    out_specs = P("rep", "state")
    return jax.shard_map(
        on_device, mesh=mesh, in_specs=in_specs, out_specs=out_specs, check_vma=False
    )
```

profile of v0, /device:TPU:1, one launch (start us, length us, event | category | flops | bytes accessed | tf_op | source)
XLA Modules:
  0.0 1223.4 jit_solution(12178156505421702784)
XLA Ops:
  6.5 0.9 slice_convert_fusion
  7.5 1.0 convert_add_fusion
  8.5 1.0 compare_and_fusion
  9.4 1.5 copy.5
  11.8 111.1 %psum.84 = f32[64,8]{0,1:T(8,128)S(1)} all-reduce(f32[64,8]{0,1:T(8,128)S(1)} %dynamic_update_slice.18), channel_id=1, replica_groups=mesh['state'=128,'rep'=4] {'state','rep'}, use_global_device_ids=true, to_apply=%region_0.2 | all-reduce | flops 512 | bytes 4096 | tf_op jit(solution)/shard_map/psum | solution.py:96
  124.1 0.7 multiply_reduce_fusion.47
  124.8 0.7 fusion.365
  127.4 0.7 fusion.364
  129.0 0.6 slice_reduce_fusion.46
  130.3 0.6 multiply_reduce_fusion.46
  142.4 0.6 slice_reduce_fusion.43
  143.6 0.6 multiply_reduce_fusion.43
  147.1 0.6 slice_reduce_fusion.42
  148.4 0.6 multiply_reduce_fusion.42
  152.0 0.7 slice_reduce_fusion.41
  153.4 0.7 multiply_reduce_fusion.41
  157.0 0.7 slice_reduce_fusion.40
  158.4 0.7 multiply_reduce_fusion.40
  161.7 1.0 fusion.260
  162.8 0.7 fusion.362
  163.5 0.7 fusion.363
  164.3 0.7 fusion.360
  165.6 0.9 fusion.53
  167.0 0.7 fusion.361
  167.8 42.7 %all-reduce.7.cloned.1.call-done = f32[8,4096]{1,0:T(8,128)} async-done(((f32[8,4096]{1,0:T(8,128)}), f32[8,4096]{1,0:T(8,128)}) %all-reduce.7.cloned.1.call-update) | async-done | bytes 131088 | tf_op jit(solution)/shard_map/psum | solution.py:105
  210.5 2.3 fusion.359
  217.1 106.1 %psum.86 = f32[64,8]{0,1:T(8,128)S(1)} all-reduce(f32[64,8]{0,1:T(8,128)S(1)} %dynamic_update_slice.19), channel_id=1, replica_groups=mesh['state'=128,'rep'=4] {'state','rep'}, use_global_device_ids=true, to_apply=%region_18.20 | all-reduce | flops 512 | bytes 4096 | tf_op jit(solution)/shard_map/psum | solution.py:96
  327.9 0.6 slice_reduce_fusion.38
  332.7 0.6 slice_reduce_fusion.37
  337.5 0.6 slice_reduce_fusion.36
  342.1 0.6 slice_reduce_fusion.35
  360.8 1.0 fusion.250
  362.7 48.0 %all-reduce.9.cloned.1.call-done = f32[8,4096]{1,0:T(8,128)} async-done(((f32[8,4096]{1,0:T(8,128)}), f32[8,4096]{1,0:T(8,128)}) %all-reduce.9.cloned.1.call-update) | async-done | bytes 131088 | tf_op jit(solution)/shard_map/psum | solution.py:105
  410.7 2.3 fusion.358
  417.3 106.1 %psum.88 = f32[64,8]{0,1:T(8,128)S(1)} all-reduce(f32[64,8]{0,1:T(8,128)S(1)} %dynamic_update_slice.20), channel_id=1, replica_groups=mesh['state'=128,'rep'=4] {'state','rep'}, use_global_device_ids=true, to_apply=%region_36.38 | all-reduce | flops 512 | bytes 4096 | tf_op jit(solution)/shard_map/psum | solution.py:96
  528.2 0.6 slice_reduce_fusion.30
  532.8 0.6 slice_reduce_fusion.29
  537.4 0.6 slice_reduce_fusion.28
  542.2 0.6 slice_reduce_fusion.27
  560.8 1.0 fusion.240
  562.6 48.0 %all-reduce.11.cloned.1.call-done = f32[8,4096]{1,0:T(8,128)} async-done(((f32[8,4096]{1,0:T(8,128)}), f32[8,4096]{1,0:T(8,128)}) %all-reduce.11.cloned.1.call-update) | async-done | bytes 131088 | tf_op jit(solution)/shard_map/psum | solution.py:105
  610.6 2.4 fusion.357
  617.3 106.1 %psum.90 = f32[64,8]{0,1:T(8,128)S(1)} all-reduce(f32[64,8]{0,1:T(8,128)S(1)} %dynamic_update_slice.21), channel_id=1, replica_groups=mesh['state'=128,'rep'=4] {'state','rep'}, use_global_device_ids=true, to_apply=%region_54.56 | all-reduce | flops 512 | bytes 4096 | tf_op jit(solution)/shard_map/psum | solution.py:96
  728.1 0.6 slice_reduce_fusion.22
  732.8 0.6 slice_reduce_fusion.21
  737.4 0.6 slice_reduce_fusion.20
  760.9 1.0 fusion.230
  762.9 47.8 %all-reduce.13.cloned.1.call-done = f32[8,4096]{1,0:T(8,128)} async-done(((f32[8,4096]{1,0:T(8,128)}), f32[8,4096]{1,0:T(8,128)}) %all-reduce.13.cloned.1.call-update) | async-done | bytes 131088 | tf_op jit(solution)/shard_map/psum | solution.py:105
  810.7 2.4 fusion.356
  817.3 106.1 %psum.92 = f32[64,8]{0,1:T(8,128)S(1)} all-reduce(f32[64,8]{0,1:T(8,128)S(1)} %dynamic_update_slice.22), channel_id=1, replica_groups=mesh['state'=128,'rep'=4] {'state','rep'}, use_global_device_ids=true, to_apply=%region_72.74 | all-reduce | flops 512 | bytes 4096 | tf_op jit(solution)/shard_map/psum | solution.py:96
  928.0 0.6 slice_reduce_fusion.14
  932.7 0.6 slice_reduce_fusion.13
  937.5 0.6 slice_reduce_fusion.12
  960.9 1.0 fusion.220
  962.7 48.1 %all-reduce.15.cloned.1.call-done = f32[8,4096]{1,0:T(8,128)} async-done(((f32[8,4096]{1,0:T(8,128)}), f32[8,4096]{1,0:T(8,128)}) %all-reduce.15.cloned.1.call-update) | async-done | bytes 131088 | tf_op jit(solution)/shard_map/psum | solution.py:105
  1010.8 2.4 fusion.355
  1017.4 106.4 %psum.94 = f32[64,8]{0,1:T(8,128)S(1)} all-reduce(f32[64,8]{0,1:T(8,128)S(1)} %dynamic_update_slice.23), channel_id=1, replica_groups=mesh['state'=128,'rep'=4] {'state','rep'}, use_global_device_ids=true, to_apply=%region_90.92 | all-reduce | flops 512 | bytes 4096 | tf_op jit(solution)/shard_map/psum | solution.py:96
  1128.5 0.6 slice_reduce_fusion.6
  1133.1 0.6 slice_reduce_fusion.5
  1137.6 0.6 slice_reduce_fusion.4
  1160.9 1.0 fusion.210
  1162.5 48.2 %all-reduce.17.cloned.1.call-done = f32[8,4096]{1,0:T(8,128)} async-done(((f32[8,4096]{1,0:T(8,128)}), f32[8,4096]{1,0:T(8,128)}) %all-reduce.17.cloned.1.call-update) | async-done | bytes 131088 | tf_op jit(solution)/shard_map/psum | solution.py:105
  1210.7 2.2 fusion.354
  1215.3 1.2 convolution_add_fusion
  (385 shorter events, 79.7 us)
Async XLA Ops:
  6.5 155.2 %copy-start = (f32[16,4096]{1,0:T(8,128)S(1)}, f32[16,4096]{1,0:T(8,128)}, u32[]{:S(2)}) copy-start(f32[16,4096]{1,0:T(8,128)} %param.6) | copy-start | bytes 786436
  6.5 118.3 %copy-start.2 = (f32[48]{0:T(128)S(1)}, f32[48]{0:T(128)}, u32[]{:S(2)}) copy-start(f32[48]{0:T(128)} %param.8) | copy-start | bytes 580
  6.5 120.8 %copy-start.1 = (f32[48]{0:T(128)S(1)}, f32[48]{0:T(128)}, u32[]{:S(2)}) copy-start(f32[48]{0:T(128)} %param.7) | copy-start | bytes 580
  6.5 204.0 %all-reduce.7.cloned.1.call-start = ((), (), s32[]{:S(2)}) async-start(), calls=%async_computation | async-start | bytes 262144 | tf_op jit(solution)/shard_map/psum | solution.py:105
  162.7 247.9 %all-reduce.9.cloned.1.call-start = ((), (), s32[]{:S(2)}) async-start(), calls=%async_computation.1 | async-start | bytes 262144 | tf_op jit(solution)/shard_map/psum | solution.py:105
  361.8 248.9 %all-reduce.11.cloned.1.call-start = ((), (), s32[]{:S(2)}) async-start(), calls=%async_computation.2 | async-start | bytes 262144 | tf_op jit(solution)/shard_map/psum | solution.py:105
  561.8 248.8 %all-reduce.13.cloned.1.call-start = ((), (), s32[]{:S(2)}) async-start(), calls=%async_computation.3 | async-start | bytes 262144 | tf_op jit(solution)/shard_map/psum | solution.py:105
  761.9 248.9 %all-reduce.15.cloned.1.call-start = ((), (), s32[]{:S(2)}) async-start(), calls=%async_computation.4 | async-start | bytes 262144 | tf_op jit(solution)/shard_map/psum | solution.py:105
  962.0 248.8 %all-reduce.17.cloned.1.call-start = ((), (), s32[]{:S(2)}) async-start(), calls=%async_computation.5 | async-start | bytes 262144 | tf_op jit(solution)/shard_map/psum | solution.py:105
Sparse Core Ops, SparseCore 0:
  162.9 47.6 all-reduce.6
  361.9 48.7 all-reduce.8
  561.9 48.6 all-reduce.10
  762.0 48.6 all-reduce.12
  962.1 48.6 all-reduce.14
  1162.0 48.6 all-reduce.16
where the time goes:
time: 1230 us; the launch traced here: 1220 us
  blocking collectives  642 us (52%)
  waiting for transfers between devices  283 us (23%)
  between operations  171 us (14%)
  other arithmetic  81.6 us (7%)
  matrix products  24.9 us (2%)
  local copies, waits for them, and re-layouts  20.7 us (2%)
    psum x6, blocking collectives, on_device(): lax.psum(picked(current, block_locs, column_start, rep_index), ('state',...  642 us
    psum x6, waiting for transfers between devices, on_device(): projected = lax.psum(partial_value, 'rep')  283 us
    reduce_sum x48, other arithmetic, block_factors(): mean_value = jnp.mean(prior_col)  29.5 us
    reduce_sum x48, other arithmetic, block_factors(): variance = jnp.sum(spread * spread) / (M - 1)  29.2 us
  transfers between devices with their start and end apart: 6, of which 6 were waited for; matrix products, arithmetic and copies ran while one was open for 1% of the time, Pallas kernels for 0%

commit v1 on v0

v1 whole, which is shorter than its diff:
```python
import functools

import jax
import jax.numpy as jnp
from jax import lax
from jax.experimental import pallas as pl
from jax.experimental.pallas import tpu as pltpu
from jax.sharding import PartitionSpec as P

MESH = pl.DeviceIdType.MESH
M = 64
TILE = 128
HALF = 4096
REACH = 2 * HALF
LINK = REACH + TILE // 2
NOBS = 48
REPS = 4
CORES = 2
WINDOW = 4
SLOTS = 8
CHUNKS = 4
ROWS = (2 * WINDOW + 1) * CORES * REPS


def taper(distance):
    ratio = distance * (1.0 / HALF)
    near_part = (((-0.25 * ratio + 0.5) * ratio + 0.625) * ratio - 5.0 / 3.0) * ratio * ratio + 1.0
    ratio_far = jnp.maximum(ratio, 1.0)
    far_part = (
        ((((ratio_far / 12.0 - 0.5) * ratio_far + 0.625) * ratio_far + 5.0 / 3.0) * ratio_far - 5.0)
        * ratio_far
        + 4.0
        - 2.0 / (3.0 * ratio_far)
    )
    return jnp.where(
        ratio <= 1.0, near_part, jnp.where(ratio < 2.0, far_part, jnp.zeros_like(ratio))
    )


def iota(shape, axis):
    return lax.broadcasted_iota(jnp.int32, shape, axis)


def gather_kernel(
    chips, held, loc_ref, ens_ref, rows_ref, all_ref, far_ref,
    local_ref, pick_ref, local_sem, own_sem, row_send, row_recv,
    send_right, send_left, recv_left, recv_right, pass_right, pass_left, far_left, far_right,
):
    state = lax.axis_index("state")
    rep = lax.axis_index("rep")
    chip = state // CORES
    core = state % CORES
    part_rows = ens_ref.shape[0]

    def partner(index):
        shift = index // (CORES * REPS) - WINDOW
        other_core = (core + (index // REPS) % CORES) % CORES
        other_rep = (rep + index % REPS) % REPS
        other_chip = (chip + shift + chips) % chips
        return shift, (other_chip * CORES + other_core, other_rep)

    itself = WINDOW * CORES * REPS
    tiles = held // TILE

    def load(tile):
        span = pl.ds(pl.multiple_of(tile * TILE, TILE), TILE)
        return pltpu.make_async_copy(ens_ref.at[:, span], local_ref.at[tile], local_sem)

    def fetch(tile, carry):
        load(tile).start()
        return carry

    lax.fori_loop(0, tiles, fetch, 0)
    barrier = pltpu.get_barrier_semaphore()

    def greet(index, carry):
        _, target = partner(index)
        pl.semaphore_signal(barrier, inc=1, device_id=target, device_id_type=MESH)
        return carry

    lax.fori_loop(0, itself, greet, 0)
    lax.fori_loop(itself + 1, ROWS, greet, 0)
    pltpu.make_async_copy(local_ref, local_ref, local_sem).wait()

    lane = iota((part_rows, TILE), 1)
    diagonal = lane - iota((part_rows, TILE), 0)

    def pick(j, carry):
        rank, packed = carry
        offset = loc_ref[j] - state * held
        inside = (offset >= 0) & (offset < held)
        safe = jnp.clip(offset, 0, held - 1)
        tile = local_ref[safe // TILE]
        wanted = jnp.where(inside, safe % TILE, -1)
        column = jnp.sum(jnp.where(lane == wanted, tile, 0.0), axis=1, keepdims=True)
        place = jnp.where(inside, rank * part_rows, -TILE * 2)
        packed = jnp.where(diagonal == place, column, packed)
        return rank + inside.astype(jnp.int32), packed

    _, packed = lax.fori_loop(
        0, NOBS, pick, (jnp.int32(0), jnp.zeros((part_rows, TILE), jnp.float32))
    )
    pick_ref[0] = jnp.sum(packed, axis=0, keepdims=True)

    pl.semaphore_wait(barrier, ROWS - 1)

    def row_copy(index):
        shift, target = partner(index)
        slot = ((WINDOW - shift) * CORES + core) * REPS + rep
        return pltpu.make_async_remote_copy(
            src_ref=pick_ref.at[0],
            dst_ref=rows_ref.at[slot],
            send_sem=row_send,
            recv_sem=row_recv,
            device_id=target,
            device_id_type=MESH,
        )

    def send_row(index, carry):
        row_copy(index).start()
        return carry

    lax.fori_loop(0, itself, send_row, 0)
    lax.fori_loop(itself + 1, ROWS, send_row, 0)
    own = pltpu.make_async_copy(
        pick_ref.at[0], rows_ref.at[(WINDOW * CORES + core) * REPS + rep], own_sem
    )
    own.start()

    right = (state, (rep + 1) % REPS)
    left = (state, (rep + REPS - 1) % REPS)
    width = held // CHUNKS

    def piece(ref, chunk):
        return ref.at[:, pl.ds(chunk * width, width)]

    def bulk(source, owner, chunk, target, send_sem, recv_sem):
        return pltpu.make_async_remote_copy(
            src_ref=piece(source, chunk),
            dst_ref=piece(all_ref.at[owner], chunk),
            send_sem=send_sem.at[chunk],
            recv_sem=recv_sem.at[chunk],
            device_id=target,
            device_id_type=MESH,
        )

    half = CHUNKS // 2
    to_right = [bulk(ens_ref, rep, c, right, send_right, recv_left) for c in range(CHUNKS)]
    to_left = [bulk(ens_ref, rep, c, left, send_left, recv_right) for c in range(CHUNKS)]
    for step in range(CHUNKS):
        to_right[step].start()
        to_left[(step + half) % CHUNKS].start()

    shards = iota((8, TILE), 1)
    first = shards * held

    def reach(i, carry):
        low, high, count, far = carry
        spot = loc_ref[NOBS - 1 - i]
        near = (spot >= low) & (spot <= high)
        away = jnp.abs(spot // (held * CORES) - shards // CORES) > WINDOW
        count = count + (spot // held == shards).astype(jnp.int32)
        far = jnp.where((near & away) | (count > SLOTS), 1, far)
        low = jnp.where(near, jnp.minimum(low, spot - LINK), low)
        high = jnp.where(near, jnp.maximum(high, spot + LINK), high)
        return low, high, count, far

    zeros = jnp.zeros((8, TILE), jnp.int32)
    far = lax.fori_loop(
        0, NOBS, reach, (first - REACH, first + held + REACH, zeros, zeros)
    )[3]
    far_ref[0, 0] = jnp.max(far)

    left_rep, right_rep, across = left[1], right[1], (rep + 2) % REPS
    relays = []
    for step in range(half):
        to_right[step].wait_recv()
        relay = bulk(all_ref.at[left_rep], left_rep, step, right, pass_right, far_left)
        relay.start()
        relays.append(relay)
        to_left[half + step].wait_recv()
        relay = bulk(all_ref.at[right_rep], right_rep, half + step, left, pass_left, far_right)
        relay.start()
        relays.append(relay)
    for step in range(half):
        to_right[half + step].wait_recv()
        to_left[step].wait_recv()
    for relay in relays:
        relay.wait()
    for copy in to_right + to_left:
        copy.wait_send()
    own.wait()
    pltpu.make_async_copy(
        rows_ref.at[pl.ds(0, ROWS - 1)], rows_ref.at[pl.ds(0, ROWS - 1)], row_send
    ).wait()
    pltpu.make_async_copy(
        rows_ref.at[pl.ds(0, ROWS - 1)], rows_ref.at[pl.ds(0, ROWS - 1)], row_recv
    ).wait()


def gather(mesh, ensemble, locations):
    part_rows, held = ensemble.shape
    dma = pltpu.SemaphoreType.DMA
    return pl.pallas_call(
        functools.partial(gather_kernel, mesh.shape["state"] // CORES, held),
        out_shape=(
            jax.ShapeDtypeStruct((ROWS, 1, TILE), jnp.float32),
            jax.ShapeDtypeStruct((REPS, part_rows, held), jnp.float32),
            jax.ShapeDtypeStruct((1, 1), jnp.int32),
        ),
        in_specs=[pl.BlockSpec(memory_space=pltpu.SMEM), pl.BlockSpec(memory_space=pl.ANY)],
        out_specs=(
            pl.BlockSpec(memory_space=pl.ANY),
            pl.BlockSpec(memory_space=pl.ANY),
            pl.BlockSpec(memory_space=pltpu.SMEM),
        ),
        scratch_shapes=[
            pltpu.VMEM((held // TILE, part_rows, TILE), jnp.float32),
            pltpu.VMEM((1, 1, TILE), jnp.float32),
            dma, dma, dma, dma,
            dma((CHUNKS,)), dma((CHUNKS,)), dma((CHUNKS,)), dma((CHUNKS,)),
            dma((CHUNKS,)), dma((CHUNKS,)), dma((CHUNKS,)), dma((CHUNKS,)),
        ],
        compiler_params=pltpu.CompilerParams(collective_id=0, has_side_effects=True),
        name="gather",
    )(locations, ensemble)


def solve_kernel(
    windowed, held, loc_ref, val_ref, err_ref, rows_ref, ens_ref, all_ref, out_ref,
    s_ref, y_ref, u_ref, w_ref, center_ref, mutual_ref, tile_ref,
    flag_ref, list_ref, slot_ref, direct_ref, count_ref, load_sem, out_sem,
):
    state = lax.axis_index("state")
    rep = lax.axis_index("rep")
    chip = state // CORES
    part_rows = ens_ref.shape[0]

    def rows_of(index):
        return pl.ds(pl.multiple_of(index * part_rows, part_rows), part_rows)

    loads = [pltpu.make_async_copy(ens_ref, s_ref.at[rows_of(rep)], load_sem.at[0])]
    for step in range(1, REPS):
        other = (rep + step) % REPS
        loads.append(
            pltpu.make_async_copy(all_ref.at[other], s_ref.at[rows_of(other)], load_sem.at[step])
        )
    for load in loads:
        load.start()

    low_own = state * held - REACH
    high_own = state * held + held + REACH

    def mark(i, carry):
        low, high = carry
        j = NOBS - 1 - i
        spot = loc_ref[j]
        near = (spot >= low) & (spot <= high)
        flag_ref[j] = near.astype(jnp.int32)
        count_ref[spot // held] = 0
        low = jnp.where(near, jnp.minimum(low, spot - LINK), low)
        high = jnp.where(near, jnp.maximum(high, spot + LINK), high)
        return low, high

    lax.fori_loop(0, NOBS, mark, (low_own, high_own))

    def enlist(j, carry):
        total, direct = carry
        spot = loc_ref[j]
        shard = spot // held
        rank = count_ref[shard]
        count_ref[shard] = rank + 1
        list_ref[total] = j
        slot_ref[total] = rank
        direct_ref[direct] = total
        touches = (spot >= low_own) & (spot <= high_own)
        return total + flag_ref[j], direct + touches.astype(jnp.int32)

    total, direct = lax.fori_loop(0, NOBS, enlist, (jnp.int32(0), jnp.int32(0)))

    diagonal = iota((part_rows, TILE), 1) - iota((part_rows, TILE), 0)

    def spread(t, carry):
        j = list_ref[t]
        spot = loc_ref[j]
        shard = spot // held
        if windowed:
            base = ((shard // CORES - chip + WINDOW) * CORES + shard % CORES) * REPS
            place = slot_ref[t] * part_rows
        else:
            base = j * REPS
            place = 0
        for r in range(REPS):
            row = jnp.broadcast_to(rows_ref[base + r], (part_rows, TILE))
            column = jnp.sum(jnp.where(diagonal == place, row, 0.0), axis=1, keepdims=True)
            y_ref[t, r * part_rows : (r + 1) * part_rows, :] = jnp.broadcast_to(
                column, (part_rows, TILE)
            )
        center = (spot // TILE * TILE).astype(jnp.float32) + (TILE - 1) * 0.5
        center_ref[pl.ds(t, 1), :] = jnp.full((1, TILE), center, jnp.float32)
        return carry

    lax.fori_loop(0, total, spread, 0)

    tiles = held // TILE
    tile_centers = (state * held + iota((tiles, TILE), 0) * TILE).astype(jnp.float32) + (
        TILE - 1
    ) * 0.5

    def assimilate(t, carry):
        j = list_ref[t]
        spot = loc_ref[j].astype(jnp.float32)
        error = err_ref[j]
        y = y_ref[t]
        mean = jnp.sum(y, axis=0, keepdims=True) * (1.0 / M)
        spread_of = y - mean
        variance = jnp.sum(spread_of * spread_of, axis=0, keepdims=True) * (1.0 / (M - 1))
        total_var = variance + error
        shrink = 1.0 / (1.0 + jnp.sqrt(error / total_var))
        u = spread_of * (1.0 / ((M - 1) * total_var))
        w = (val_ref[j] - mean) - shrink * spread_of
        u_ref[t] = u
        w_ref[t] = w
        mutual_ref[...] = taper(jnp.abs(center_ref[...] - spot))
        tile_ref[t] = taper(jnp.abs(tile_centers - spot))

        def update(k, inner):
            other = y_ref[k]
            projected = jnp.sum(u * other, axis=0, keepdims=True)
            y_ref[k] = other + w * (mutual_ref[pl.ds(k, 1), :] * projected)
            return inner

        lax.fori_loop(t + 1, total, update, 0)
        return carry

    lax.fori_loop(0, total, assimilate, 0)

    for load in loads:
        load.wait()
    group = 4

    def apply(g, carry):
        spans = [
            pl.ds(pl.multiple_of((g * group + i) * TILE, TILE), TILE) for i in range(group)
        ]

        def one(d, values):
            t = direct_ref[d]
            u = u_ref[t]
            w = w_ref[t]
            result = []
            for i in range(group):
                projected = jnp.sum(u * values[i], axis=0, keepdims=True)
                weight = tile_ref[t, pl.ds(g * group + i, 1), :]
                result.append(values[i] + w * (weight * projected))
            return tuple(result)

        values = lax.fori_loop(0, direct, one, tuple(s_ref[:, span] for span in spans))
        for span, value in zip(spans, values):
            s_ref[:, span] = value
        return carry

    lax.fori_loop(0, tiles // group, apply, 0)
    store = pltpu.make_async_copy(s_ref.at[rows_of(rep)], out_ref, out_sem)
    store.start()
    store.wait()


def solve(windowed, ensemble, values, errors, locations, rows, everything):
    part_rows, held = ensemble.shape
    smem = pl.BlockSpec(memory_space=pltpu.SMEM)
    anywhere = pl.BlockSpec(memory_space=pl.ANY)
    block = pltpu.VMEM((NOBS, M, TILE), jnp.float32)
    return pl.pallas_call(
        functools.partial(solve_kernel, windowed, held),
        out_shape=jax.ShapeDtypeStruct((part_rows, held), jnp.float32),
        in_specs=[smem, smem, smem, pl.BlockSpec(memory_space=pltpu.VMEM), anywhere, anywhere],
        out_specs=anywhere,
        scratch_shapes=[
            pltpu.VMEM((M, held), jnp.float32),
            block, block, block,
            pltpu.VMEM((NOBS, TILE), jnp.float32),
            pltpu.VMEM((NOBS, TILE), jnp.float32),
            pltpu.VMEM((NOBS, held // TILE, TILE), jnp.float32),
            pltpu.SMEM((NOBS,), jnp.int32),
            pltpu.SMEM((NOBS,), jnp.int32),
            pltpu.SMEM((NOBS,), jnp.int32),
            pltpu.SMEM((NOBS,), jnp.int32),
            pltpu.SMEM((128,), jnp.int32),
            pltpu.SemaphoreType.DMA((REPS,)),
            pltpu.SemaphoreType.DMA,
        ],
        name="solve",
    )(locations, values, errors, rows, ensemble, everything)


def full_rows(mesh, ensemble, locations):
    part_rows, held = ensemble.shape
    states = mesh.shape["state"]
    offsets = locations - lax.axis_index("state") * held
    inside = ((offsets >= 0) & (offsets < held)).astype(jnp.float32)
    columns = jnp.take(ensemble, jnp.clip(offsets, 0, held - 1), axis=1) * inside[None, :]
    placed = jnp.zeros((REPS, part_rows, NOBS), jnp.float32)
    placed = lax.dynamic_update_slice(placed, columns[None], (lax.axis_index("rep"), 0, 0))
    stride = 1
    while stride < states:
        pairs = [(i, i ^ stride) for i in range(states)]
        placed = placed + lax.ppermute(placed, "state", pairs)
        stride *= 2
    stride = 1
    while stride < REPS:
        pairs = [(i, i ^ stride) for i in range(REPS)]
        placed = placed + lax.ppermute(placed, "rep", pairs)
        stride *= 2
    by_obs = jnp.transpose(placed, (2, 0, 1)).reshape(NOBS * REPS, 1, part_rows)
    return jnp.pad(by_obs, ((0, 0), (0, 0), (0, TILE - part_rows)))


def on_device(mesh, ensemble, obs_values, obs_error, obs_location):
    rows, everything, far = gather(mesh, ensemble, obs_location)
    return lax.cond(
        far[0, 0] == 0,
        lambda: solve(True, ensemble, obs_values, obs_error, obs_location, rows, everything),
        lambda: solve(
            False, ensemble, obs_values, obs_error, obs_location,
            full_rows(mesh, ensemble, obs_location), everything,
        ),
    )


def solution(mesh):
    in_specs = (P("rep", "state"), P(), P(), P())
    out_specs = P("rep", "state")
    return jax.shard_map(
        functools.partial(on_device, mesh),
        mesh=mesh,
        in_specs=in_specs,
        out_specs=out_specs,
        check_vma=False,
    )
```

time: 1230 us -> 38.1 us (0.03)
  blocking collectives: 642 us -> 0 us
  waiting for transfers between devices: 283 us -> 0 us
  between operations: 171 us -> 0.71 us
  other arithmetic: 81.6 us -> 0 us
  Pallas kernels: 0 us -> 36.6 us
  matrix products: 24.9 us -> 0 us
  local copies, waits for them, and re-layouts: 20.7 us -> 0.7 us
    psum x6 -> x0, blocking collectives: 642 us -> none  [on_device(): lax.psum(picked(current, block_locs, column_start, rep_index), ('state',...]
    psum x6 -> x0, waiting for transfers between devices: 283 us -> none  [on_device(): projected = lax.psum(partial_value, 'rep')]
    reduce_sum x96 -> x0, other arithmetic: 58.8 us -> none  [the longest x48 29.5 us: block_factors(): mean_value = jnp.mean(prior_col)]
    pallas_call x0 -> x2, Pallas kernels: none -> 36.6 us  [the longest x1 33.6 us: gather(): pl.pallas_call(functools.partial(gather_kernel, mesh.shape['state'] // CO...]
    dot_general x96 -> x0, matrix products: 24.9 us -> none  [the longest x36 9.32 us: solve_scaled(): jnp.dot(mixing[:slot, slot], jnp.stack(scaled), precision=lax.Precision.H...]
    slice x6 -> x0, other arithmetic: 14 us -> none  [solve_scaled(): running = projected[slot]]
  transfers between devices with their start and end apart: 6 -> 0, of which waited for: 6 -> 0; matrix products, arithmetic and copies ran while one was open for 1% -> 0% of each run, Pallas kernels for 0% -> 0%
where the time goes in v1:
time: 38.1 us; the launch traced here: 38 us
  Pallas kernels  36.6 us (96%)
  between operations  0.71 us (2%)
  local copies, waits for them, and re-layouts  0.7 us (2%)
    pallas_call x1, Pallas kernels, gather(): pl.pallas_call(functools.partial(gather_kernel, mesh.shape['state'] // CO...  33.6 us
    pallas_call x1, Pallas kernels, solve(): pl.pallas_call(functools.partial(solve_kernel, windowed, held), out_shape...  2.95 us

profile of v1, /device:TPU:1, one launch (start us, length us, event | category | flops | bytes accessed | tf_op | source)
XLA Modules:
  0.0 38.0 jit_solution(10040879351023609363)
XLA Ops:
  0.0 33.6 %gather.9 = (f32[72,1,128]{2,1,0:T(1,128)S(1)}, f32[4,16,4096]{2,1,0:T(8,128)S(1)}, s32[1,1]{1,0:T(1,128)}) custom-call(s32[48]{0:T(128)} %loc_ref.1, f32[16,4096]{1,0:T(8,128)} %ens_ref.1), custom_call_target="tpu_custom_call" | custom-call | tf_op jit(solution)/shard_map/gather/pallas_call | solution.py:204
  34.3 3.0 %conditional.1 = (f32[16,4096]{1,0:T(8,128)S(1)}) conditional(s32[]{:T(128)} %bitcast.5, (s32[48]{0:T(128)}, f32[16,4096]{1,0:T(8,128)}, f32[48]{0:T(128)}, f32[48]{0:T(128)}, f32[4,16,4096]{2,1,0:T(8,128)S(1)}) %tuple.11, (s32[48]{0:T(128)}, f32[48]{0:T(128)}, f32[48]{0:T(128)}, f32[72,1,128]{2,1,0:T(1,128)S(1)}, f32[16,4096]{1,0:T(8,128)}, ...), branch_computations={%region_0.1_spmd, %region_1.2_spmd} | conditional | flops 30025 | bytes 2596678 | solution.py:421
  34.3 3.0 %solve.3 = f32[16,4096]{1,0:T(8,128)S(1)} custom-call(s32[48]{0:T(128)} %get-tuple-element.35.loc_ref, f32[48]{0:T(128)} %get-tuple-element.36.val_ref, f32[48]{0:T(128)} %get-tuple-element.37.err_ref, f32[72,1,128]{2,1,0:T(1,128)S(1)} %get-tuple-element.38.rows_ref, f32[16,4096]{1,0:T(8,128)} %get-tuple-element.39.ens_ref, ...), custom_call_target="tpu_custom_call" | custom-call | tf_op jit(solution)/shard_map/cond/branch_1_fun/solve/pallas_call | solution.py:374
  37.3 0.0 copy-start.1
  37.3 0.7 %copy-done.1 = f32[16,4096]{1,0:T(8,128)} copy-done((f32[16,4096]{1,0:T(8,128)}, f32[16,4096]{1,0:T(8,128)S(1)}, u32[]{:S(2)}) %copy-start.1) | copy-done | bytes 262168
Async XLA Ops:
  37.3 0.7 %copy-start.1 = (f32[16,4096]{1,0:T(8,128)}, f32[16,4096]{1,0:T(8,128)S(1)}, u32[]{:S(2)}) copy-start(f32[16,4096]{1,0:T(8,128)S(1)} %get-tuple-element.60) | copy-start | bytes 786436

commit v2 on v1

--- a/solution.py
+++ b/solution.py
@@ -17,6 +17,7 @@
 REPS = 4
 CORES = 2
 WINDOW = 4
+DEPTH = 16
 SLOTS = 8
 CHUNKS = 4
 ROWS = (2 * WINDOW + 1) * CORES * REPS
@@ -43,92 +44,103 @@
 
 def gather_kernel(
     chips, held, loc_ref, ens_ref, rows_ref, all_ref, far_ref,
-    local_ref, pick_ref, local_sem, own_sem, row_send, row_recv,
+    local_ref, pick_ref, local_sem, own_sem, late_sem, row_send, row_recv,
     send_right, send_left, recv_left, recv_right, pass_right, pass_left, far_left, far_right,
 ):
     state = lax.axis_index("state")
     rep = lax.axis_index("rep")
-    chip = state // CORES
-    core = state % CORES
+    chip = state >> 1
+    core = state & 1
     part_rows = ens_ref.shape[0]
-
-    def partner(index):
-        shift = index // (CORES * REPS) - WINDOW
-        other_core = (core + (index // REPS) % CORES) % CORES
-        other_rep = (rep + index % REPS) % REPS
-        other_chip = (chip + shift + chips) % chips
-        return shift, (other_chip * CORES + other_core, other_rep)
-
-    itself = WINDOW * CORES * REPS
     tiles = held // TILE
 
     def load(tile):
         span = pl.ds(pl.multiple_of(tile * TILE, TILE), TILE)
         return pltpu.make_async_copy(ens_ref.at[:, span], local_ref.at[tile], local_sem)
 
-    def fetch(tile, carry):
+    for tile in range(tiles):
         load(tile).start()
-        return carry
-
-    lax.fori_loop(0, tiles, fetch, 0)
+
+    depth = chip & (DEPTH - 1)
+    shifts = [shift for shift in range(-WINDOW, WINDOW + 1) if shift != 0]
+    valid = {n: (chip + n >= 0) & (chip + n < chips) for n in shifts}
+    ahead = {n: (depth + n < DEPTH) if n > 0 else (depth + n < 0) for n in shifts}
+    later = {n: valid[n] & ahead[n] for n in shifts}
+    earlier = {n: valid[n] & jnp.logical_not(ahead[n]) for n in shifts}
+    members = [(c, r) for c in range(CORES) for r in range(REPS)]
+    beside = members[1:]
+    cores_of = [core, 1 - core]
+    reps_of = [(rep + r) & (REPS - 1) for r in range(REPS)]
+
+    def target(shift, member):
+        return (chip + shift) * CORES + cores_of[member[0]], reps_of[member[1]]
+
+    def signal(semaphore, shift, member):
+        pl.semaphore_signal(
+            semaphore, inc=1, device_id=target(shift, member), device_id_type=MESH
+        )
+
+    def count_of(flags):
+        return sum(flags[n].astype(jnp.int32) for n in shifts) * len(members)
+
     barrier = pltpu.get_barrier_semaphore()
-
-    def greet(index, carry):
-        _, target = partner(index)
-        pl.semaphore_signal(barrier, inc=1, device_id=target, device_id_type=MESH)
-        return carry
-
-    lax.fori_loop(0, itself, greet, 0)
-    lax.fori_loop(itself + 1, ROWS, greet, 0)
+    for member in beside:
+        signal(barrier, 0, member)
+    for n in shifts:
+
+        @pl.when(later[n])
+        def _(n=n):
+            for member in members:
+                signal(barrier, n, member)
+
     pltpu.make_async_copy(local_ref, local_ref, local_sem).wait()
-
     lane = iota((part_rows, TILE), 1)
     diagonal = lane - iota((part_rows, TILE), 0)
-
-    def pick(j, carry):
-        rank, packed = carry
+    rank = jnp.int32(0)
+    packed = jnp.zeros((part_rows, TILE), jnp.float32)
+    for j in range(NOBS):
         offset = loc_ref[j] - state * held
         inside = (offset >= 0) & (offset < held)
         safe = jnp.clip(offset, 0, held - 1)
-        tile = local_ref[safe // TILE]
-        wanted = jnp.where(inside, safe % TILE, -1)
+        tile = local_ref[safe >> 7]
+        wanted = jnp.where(inside, safe & (TILE - 1), -1)
         column = jnp.sum(jnp.where(lane == wanted, tile, 0.0), axis=1, keepdims=True)
         place = jnp.where(inside, rank * part_rows, -TILE * 2)
         packed = jnp.where(diagonal == place, column, packed)
-        return rank + inside.astype(jnp.int32), packed
-
-    _, packed = lax.fori_loop(
-        0, NOBS, pick, (jnp.int32(0), jnp.zeros((part_rows, TILE), jnp.float32))
-    )
+        rank = rank + inside.astype(jnp.int32)
     pick_ref[0] = jnp.sum(packed, axis=0, keepdims=True)
 
-    pl.semaphore_wait(barrier, ROWS - 1)
-
-    def row_copy(index):
-        shift, target = partner(index)
+    pl.semaphore_wait(barrier, len(beside) + count_of(earlier))
+
+    def send_row(shift, member):
         slot = ((WINDOW - shift) * CORES + core) * REPS + rep
-        return pltpu.make_async_remote_copy(
+        pltpu.make_async_remote_copy(
             src_ref=pick_ref.at[0],
             dst_ref=rows_ref.at[slot],
-            send_sem=row_send,
-            recv_sem=row_recv,
-            device_id=target,
+            send_sem=row_send.at[WINDOW + shift],
+            recv_sem=row_recv.at[WINDOW - shift],
+            device_id=target(shift, member),
             device_id_type=MESH,
-        )
-
-    def send_row(index, carry):
-        row_copy(index).start()
-        return carry
-
-    lax.fori_loop(0, itself, send_row, 0)
-    lax.fori_loop(itself + 1, ROWS, send_row, 0)
+        ).start()
+
+    for n in shifts:
+
+        @pl.when(earlier[n])
+        def _(n=n):
+            for member in members:
+                signal(late_sem.at[WINDOW - n], n, member)
+            for member in members:
+                send_row(n, member)
+
+    for member in beside:
+        send_row(0, member)
     own = pltpu.make_async_copy(
         pick_ref.at[0], rows_ref.at[(WINDOW * CORES + core) * REPS + rep], own_sem
     )
     own.start()
 
-    right = (state, (rep + 1) % REPS)
-    left = (state, (rep + REPS - 1) % REPS)
+    right = (state, reps_of[1])
+    left = (state, reps_of[3])
     width = held // CHUNKS
 
     def piece(ref, chunk):
@@ -158,8 +170,8 @@
         low, high, count, far = carry
         spot = loc_ref[NOBS - 1 - i]
         near = (spot >= low) & (spot <= high)
-        away = jnp.abs(spot // (held * CORES) - shards // CORES) > WINDOW
-        count = count + (spot // held == shards).astype(jnp.int32)
+        away = jnp.abs((spot >> 13) - (shards >> 1)) > WINDOW
+        count = count + ((spot >> 12) == shards).astype(jnp.int32)
         far = jnp.where((near & away) | (count > SLOTS), 1, far)
         low = jnp.where(near, jnp.minimum(low, spot - LINK), low)
         high = jnp.where(near, jnp.maximum(high, spot + LINK), high)
@@ -167,21 +179,29 @@
 
     zeros = jnp.zeros((8, TILE), jnp.int32)
     far = lax.fori_loop(
-        0, NOBS, reach, (first - REACH, first + held + REACH, zeros, zeros)
+        0, NOBS, reach, (first - REACH, first + held + REACH, zeros, zeros), unroll=8
     )[3]
     far_ref[0, 0] = jnp.max(far)
 
-    left_rep, right_rep, across = left[1], right[1], (rep + 2) % REPS
     relays = []
     for step in range(half):
         to_right[step].wait_recv()
-        relay = bulk(all_ref.at[left_rep], left_rep, step, right, pass_right, far_left)
+        relay = bulk(all_ref.at[left[1]], left[1], step, right, pass_right, far_left)
         relay.start()
         relays.append(relay)
         to_left[half + step].wait_recv()
-        relay = bulk(all_ref.at[right_rep], right_rep, half + step, left, pass_left, far_right)
+        relay = bulk(all_ref.at[right[1]], right[1], half + step, left, pass_left, far_right)
         relay.start()
         relays.append(relay)
+
+    for n in shifts:
+
+        @pl.when(later[n])
+        def _(n=n):
+            pl.semaphore_wait(late_sem.at[WINDOW + n], len(members))
+            for member in members:
+                send_row(n, member)
+
     for step in range(half):
         to_right[half + step].wait_recv()
         to_left[step].wait_recv()
@@ -190,12 +210,19 @@
     for copy in to_right + to_left:
         copy.wait_send()
     own.wait()
-    pltpu.make_async_copy(
-        rows_ref.at[pl.ds(0, ROWS - 1)], rows_ref.at[pl.ds(0, ROWS - 1)], row_send
-    ).wait()
-    pltpu.make_async_copy(
-        rows_ref.at[pl.ds(0, ROWS - 1)], rows_ref.at[pl.ds(0, ROWS - 1)], row_recv
-    ).wait()
+
+    def drain(semaphores, shift, number):
+        block = rows_ref.at[pl.ds((WINDOW + shift) * len(members), number)]
+        pltpu.make_async_copy(block, block, semaphores.at[WINDOW + shift]).wait()
+
+    drain(row_send, 0, len(beside))
+    drain(row_recv, 0, len(beside))
+    for n in shifts:
+
+        @pl.when(valid[n])
+        def _(n=n):
+            drain(row_send, n, len(members))
+            drain(row_recv, n, len(members))
 
 
 def gather(mesh, ensemble, locations):
@@ -217,7 +244,8 @@
         scratch_shapes=[
             pltpu.VMEM((held // TILE, part_rows, TILE), jnp.float32),
             pltpu.VMEM((1, 1, TILE), jnp.float32),
-            dma, dma, dma, dma,
+            dma, dma, pltpu.SemaphoreType.REGULAR((2 * WINDOW + 1,)),
+            dma((2 * WINDOW + 1,)), dma((2 * WINDOW + 1,)),
             dma((CHUNKS,)), dma((CHUNKS,)), dma((CHUNKS,)), dma((CHUNKS,)),
             dma((CHUNKS,)), dma((CHUNKS,)), dma((CHUNKS,)), dma((CHUNKS,)),
         ],

time: 38.1 us -> 30.5 us (0.80)
  the two profiles are of different devices: /device:TPU:1 before, /device:TPU:38 now
where the time goes in v2:
time: 30.5 us; the launch traced here: 30.3 us
  Pallas kernels  28.8 us (94%)
  between operations  0.71 us (2%)
  local copies, waits for them, and re-layouts  0.7 us (2%)
    pallas_call x1, Pallas kernels, gather(): pl.pallas_call(functools.partial(gather_kernel, mesh.shape['state'] // CO...  24.7 us
    pallas_call x1, Pallas kernels, solve(): pl.pallas_call(functools.partial(solve_kernel, windowed, held), out_shape...  4.14 us
    unnamed x2, local copies, waits for them, and re-layouts  0.7 us

profile of v2, /device:TPU:38, one launch (start us, length us, event | category | flops | bytes accessed | tf_op | source)
XLA Modules:
  0.0 30.3 jit_solution(1968519963427700883)
XLA Ops:
  0.0 24.7 %gather.9 = (f32[72,1,128]{2,1,0:T(1,128)S(1)}, f32[4,16,4096]{2,1,0:T(8,128)S(1)}, s32[1,1]{1,0:T(1,128)}) custom-call(s32[48]{0:T(128)} %loc_ref.1, f32[16,4096]{1,0:T(8,128)} %ens_ref.1), custom_call_target="tpu_custom_call" | custom-call | tf_op jit(solution)/shard_map/gather/pallas_call | solution.py:231
  25.4 4.2 %conditional.1 = (f32[16,4096]{1,0:T(8,128)S(1)}) conditional(s32[]{:T(128)} %bitcast.5, (s32[48]{0:T(128)}, f32[16,4096]{1,0:T(8,128)}, f32[48]{0:T(128)}, f32[48]{0:T(128)}, f32[4,16,4096]{2,1,0:T(8,128)S(1)}) %tuple.11, (s32[48]{0:T(128)}, f32[48]{0:T(128)}, f32[48]{0:T(128)}, f32[72,1,128]{2,1,0:T(1,128)S(1)}, f32[16,4096]{1,0:T(8,128)}, ...), branch_computations={%region_0.1_spmd, %region_1.2_spmd} | conditional | flops 30025 | bytes 2596678 | solution.py:449
  25.4 4.1 %solve.3 = f32[16,4096]{1,0:T(8,128)S(1)} custom-call(s32[48]{0:T(128)} %get-tuple-element.35.loc_ref, f32[48]{0:T(128)} %get-tuple-element.36.val_ref, f32[48]{0:T(128)} %get-tuple-element.37.err_ref, f32[72,1,128]{2,1,0:T(1,128)S(1)} %get-tuple-element.38.rows_ref, f32[16,4096]{1,0:T(8,128)} %get-tuple-element.39.ens_ref, ...), custom_call_target="tpu_custom_call" | custom-call | tf_op jit(solution)/shard_map/cond/branch_1_fun/solve/pallas_call | solution.py:402
  29.6 0.0 copy-start.1
  29.6 0.7 %copy-done.1 = f32[16,4096]{1,0:T(8,128)} copy-done((f32[16,4096]{1,0:T(8,128)}, f32[16,4096]{1,0:T(8,128)S(1)}, u32[]{:S(2)}) %copy-start.1) | copy-done | bytes 262168
Async XLA Ops:
  29.6 0.7 %copy-start.1 = (f32[16,4096]{1,0:T(8,128)}, f32[16,4096]{1,0:T(8,128)S(1)}, u32[]{:S(2)}) copy-start(f32[16,4096]{1,0:T(8,128)S(1)} %get-tuple-element.60) | copy-start | bytes 786436

commit v3 on v2

--- a/solution.py
+++ b/solution.py
@@ -44,7 +44,7 @@
 
 def gather_kernel(
     chips, held, loc_ref, ens_ref, rows_ref, all_ref, far_ref,
-    local_ref, pick_ref, local_sem, own_sem, late_sem, row_send, row_recv,
+    fetch_ref, local_ref, pick_ref, local_sem, own_sem, late_sem, near_send, near_recv, row_send, row_recv,
     send_right, send_left, recv_left, recv_right, pass_right, pass_left, far_left, far_right,
 ):
     state = lax.axis_index("state")
@@ -54,12 +54,8 @@
     part_rows = ens_ref.shape[0]
     tiles = held // TILE
 
-    def load(tile):
-        span = pl.ds(pl.multiple_of(tile * TILE, TILE), TILE)
-        return pltpu.make_async_copy(ens_ref.at[:, span], local_ref.at[tile], local_sem)
-
-    for tile in range(tiles):
-        load(tile).start()
+    load = pltpu.make_async_copy(ens_ref, fetch_ref, local_sem)
+    load.start()
 
     depth = chip & (DEPTH - 1)
     shifts = [shift for shift in range(-WINDOW, WINDOW + 1) if shift != 0]
@@ -81,7 +77,7 @@
         )
 
     def count_of(flags):
-        return sum(flags[n].astype(jnp.int32) for n in shifts) * len(members)
+        return sum(flags[n].astype(jnp.int32) for n in shifts)
 
     barrier = pltpu.get_barrier_semaphore()
     for member in beside:
@@ -90,10 +86,11 @@
 
         @pl.when(later[n])
         def _(n=n):
-            for member in members:
-                signal(barrier, n, member)
-
-    pltpu.make_async_copy(local_ref, local_ref, local_sem).wait()
+            signal(barrier, n, members[0])
+
+    load.wait()
+    for tile in range(tiles):
+        local_ref[tile] = fetch_ref[:, tile * TILE : (tile + 1) * TILE]
     lane = iota((part_rows, TILE), 1)
     diagonal = lane - iota((part_rows, TILE), 0)
     rank = jnp.int32(0)
@@ -112,32 +109,36 @@
 
     pl.semaphore_wait(barrier, len(beside) + count_of(earlier))
 
-    def send_row(shift, member):
-        slot = ((WINDOW - shift) * CORES + core) * REPS + rep
+    own_row = (WINDOW * CORES + core) * REPS + rep
+    for member in beside:
         pltpu.make_async_remote_copy(
             src_ref=pick_ref.at[0],
-            dst_ref=rows_ref.at[slot],
+            dst_ref=rows_ref.at[own_row],
+            send_sem=near_send,
+            recv_sem=near_recv,
+            device_id=target(0, member),
+            device_id_type=MESH,
+        ).start()
+    own = pltpu.make_async_copy(pick_ref.at[0], rows_ref.at[own_row], own_sem)
+    own.start()
+    for n in shifts:
+
+        @pl.when(earlier[n])
+        def _(n=n):
+            signal(late_sem.at[WINDOW - n], n, members[0])
+
+    def block(shift, number=len(members)):
+        return rows_ref.at[pl.ds((WINDOW + shift) * len(members), number)]
+
+    def send_block(shift):
+        pltpu.make_async_remote_copy(
+            src_ref=block(0),
+            dst_ref=block(-shift),
             send_sem=row_send.at[WINDOW + shift],
             recv_sem=row_recv.at[WINDOW - shift],
-            device_id=target(shift, member),
+            device_id=target(shift, members[0]),
             device_id_type=MESH,
         ).start()
-
-    for n in shifts:
-
-        @pl.when(earlier[n])
-        def _(n=n):
-            for member in members:
-                signal(late_sem.at[WINDOW - n], n, member)
-            for member in members:
-                send_row(n, member)
-
-    for member in beside:
-        send_row(0, member)
-    own = pltpu.make_async_copy(
-        pick_ref.at[0], rows_ref.at[(WINDOW * CORES + core) * REPS + rep], own_sem
-    )
-    own.start()
 
     right = (state, reps_of[1])
     left = (state, reps_of[3])
@@ -162,6 +163,15 @@
     for step in range(CHUNKS):
         to_right[step].start()
         to_left[(step + half) % CHUNKS].start()
+
+    own.wait()
+    nearby = block(0, len(beside))
+    pltpu.make_async_copy(nearby, nearby, near_recv).wait()
+    for n in shifts:
+
+        @pl.when(earlier[n])
+        def _(n=n):
+            send_block(n)
 
     shards = iota((8, TILE), 1)
     first = shards * held
@@ -198,9 +208,8 @@
 
         @pl.when(later[n])
         def _(n=n):
-            pl.semaphore_wait(late_sem.at[WINDOW + n], len(members))
-            for member in members:
-                send_row(n, member)
+            pl.semaphore_wait(late_sem.at[WINDOW + n], 1)
+            send_block(n)
 
     for step in range(half):
         to_right[half + step].wait_recv()
@@ -209,20 +218,14 @@
         relay.wait()
     for copy in to_right + to_left:
         copy.wait_send()
-    own.wait()
-
-    def drain(semaphores, shift, number):
-        block = rows_ref.at[pl.ds((WINDOW + shift) * len(members), number)]
-        pltpu.make_async_copy(block, block, semaphores.at[WINDOW + shift]).wait()
-
-    drain(row_send, 0, len(beside))
-    drain(row_recv, 0, len(beside))
+    pltpu.make_async_copy(nearby, nearby, near_send).wait()
+
     for n in shifts:
 
         @pl.when(valid[n])
         def _(n=n):
-            drain(row_send, n, len(members))
-            drain(row_recv, n, len(members))
+            pltpu.make_async_copy(block(n), block(n), row_send.at[WINDOW + n]).wait()
+            pltpu.make_async_copy(block(n), block(n), row_recv.at[WINDOW + n]).wait()
 
 
 def gather(mesh, ensemble, locations):
@@ -242,10 +245,11 @@
             pl.BlockSpec(memory_space=pltpu.SMEM),
         ),
         scratch_shapes=[
+            pltpu.VMEM((part_rows, held), jnp.float32),
             pltpu.VMEM((held // TILE, part_rows, TILE), jnp.float32),
             pltpu.VMEM((1, 1, TILE), jnp.float32),
             dma, dma, pltpu.SemaphoreType.REGULAR((2 * WINDOW + 1,)),
-            dma((2 * WINDOW + 1,)), dma((2 * WINDOW + 1,)),
+            dma, dma, dma((2 * WINDOW + 1,)), dma((2 * WINDOW + 1,)),
             dma((CHUNKS,)), dma((CHUNKS,)), dma((CHUNKS,)), dma((CHUNKS,)),
             dma((CHUNKS,)), dma((CHUNKS,)), dma((CHUNKS,)), dma((CHUNKS,)),
         ],

time: 30.5 us -> 29.1 us (0.954)
  the two profiles are of different devices: /device:TPU:38 before, /device:TPU:6 now
where the time goes in v3:
time: 29.1 us; the launch traced here: 28.9 us
  Pallas kernels  27.5 us (95%)
  between operations  0.71 us (2%)
  local copies, waits for them, and re-layouts  0.7 us (2%)
    pallas_call x1, Pallas kernels, gather(): pl.pallas_call(functools.partial(gather_kernel, mesh.shape['state'] // CO...  23.6 us
    pallas_call x1, Pallas kernels, solve(): pl.pallas_call(functools.partial(solve_kernel, windowed, held), out_shape...  3.93 us
    unnamed x2, local copies, waits for them, and re-layouts  0.7 us

profile of v3, /device:TPU:6, one launch (start us, length us, event | category | flops | bytes accessed | tf_op | source)
XLA Modules:
  0.0 28.9 jit_solution(5554706832034796182)
XLA Ops:
  0.0 23.6 %gather.9 = (f32[72,1,128]{2,1,0:T(1,128)S(1)}, f32[4,16,4096]{2,1,0:T(8,128)S(1)}, s32[1,1]{1,0:T(1,128)}) custom-call(s32[48]{0:T(128)} %loc_ref.1, f32[16,4096]{1,0:T(8,128)} %ens_ref.1), custom_call_target="tpu_custom_call" | custom-call | tf_op jit(solution)/shard_map/gather/pallas_call | solution.py:234
  24.3 3.9 %conditional.1 = (f32[16,4096]{1,0:T(8,128)S(1)}) conditional(s32[]{:T(128)} %bitcast.5, (s32[48]{0:T(128)}, f32[16,4096]{1,0:T(8,128)}, f32[48]{0:T(128)}, f32[48]{0:T(128)}, f32[4,16,4096]{2,1,0:T(8,128)S(1)}) %tuple.11, (s32[48]{0:T(128)}, f32[48]{0:T(128)}, f32[48]{0:T(128)}, f32[72,1,128]{2,1,0:T(1,128)S(1)}, f32[16,4096]{1,0:T(8,128)}, ...), branch_computations={%region_0.1_spmd, %region_1.2_spmd} | conditional | flops 30025 | bytes 2596678 | solution.py:453
  24.3 3.9 %solve.3 = f32[16,4096]{1,0:T(8,128)S(1)} custom-call(s32[48]{0:T(128)} %get-tuple-element.35.loc_ref, f32[48]{0:T(128)} %get-tuple-element.36.val_ref, f32[48]{0:T(128)} %get-tuple-element.37.err_ref, f32[72,1,128]{2,1,0:T(1,128)S(1)} %get-tuple-element.38.rows_ref, f32[16,4096]{1,0:T(8,128)} %get-tuple-element.39.ens_ref, ...), custom_call_target="tpu_custom_call" | custom-call | tf_op jit(solution)/shard_map/cond/branch_1_fun/solve/pallas_call | solution.py:406
  28.2 0.0 copy-start.1
  28.2 0.7 %copy-done.1 = f32[16,4096]{1,0:T(8,128)} copy-done((f32[16,4096]{1,0:T(8,128)}, f32[16,4096]{1,0:T(8,128)S(1)}, u32[]{:S(2)}) %copy-start.1) | copy-done | bytes 262168
Async XLA Ops:
  28.2 0.7 %copy-start.1 = (f32[16,4096]{1,0:T(8,128)}, f32[16,4096]{1,0:T(8,128)S(1)}, u32[]{:S(2)}) copy-start(f32[16,4096]{1,0:T(8,128)S(1)} %get-tuple-element.60) | copy-start | bytes 786436

commit v4 on v3

--- a/solution.py
+++ b/solution.py
@@ -43,8 +43,8 @@
 
 
 def gather_kernel(
-    chips, held, loc_ref, ens_ref, rows_ref, all_ref, far_ref,
-    fetch_ref, local_ref, pick_ref, local_sem, own_sem, late_sem, near_send, near_recv, row_send, row_recv,
+    chips, held, loc_any, val_any, err_any, ens_ref, rows_ref, all_ref, table_out, far_out,
+    loc_ref, val_ref, err_ref, far_ref, table_ref, small_sem, block_sem, fetch_ref, local_ref, pick_ref, local_sem, own_sem, late_sem, near_send, near_recv, row_send, row_recv,
     send_right, send_left, recv_left, recv_right, pass_right, pass_left, far_left, far_right,
 ):
     state = lax.axis_index("state")
@@ -56,11 +56,22 @@
 
     load = pltpu.make_async_copy(ens_ref, fetch_ref, local_sem)
     load.start()
+    smalls = [
+        pltpu.make_async_copy(loc_any, loc_ref, small_sem.at[0]),
+        pltpu.make_async_copy(val_any, val_ref, small_sem.at[1]),
+        pltpu.make_async_copy(err_any, err_ref, small_sem.at[2]),
+    ]
+    for small in smalls:
+        small.start()
 
     depth = chip & (DEPTH - 1)
-    shifts = [shift for shift in range(-WINDOW, WINDOW + 1) if shift != 0]
+    shifts = list(range(1, WINDOW + 1)) + list(range(-1, -WINDOW - 1, -1))
     valid = {n: (chip + n >= 0) & (chip + n < chips) for n in shifts}
-    ahead = {n: (depth + n < DEPTH) if n > 0 else (depth + n < 0) for n in shifts}
+
+    def key(place):
+        return place + jnp.where((place >> 2) == 2, DEPTH, 0)
+
+    ahead = {n: key((depth + n) & (DEPTH - 1)) > key(depth) for n in shifts}
     later = {n: valid[n] & ahead[n] for n in shifts}
     earlier = {n: valid[n] & jnp.logical_not(ahead[n]) for n in shifts}
     members = [(c, r) for c in range(CORES) for r in range(REPS)]
@@ -88,7 +99,10 @@
         def _(n=n):
             signal(barrier, n, members[0])
 
+    smalls[0].wait()
     load.wait()
+    block_copy = pltpu.make_async_copy(fetch_ref, all_ref.at[rep], block_sem)
+    block_copy.start()
     for tile in range(tiles):
         local_ref[tile] = fetch_ref[:, tile * TILE : (tile + 1) * TILE]
     lane = iota((part_rows, TILE), 1)
@@ -173,25 +187,68 @@
         def _(n=n):
             send_block(n)
 
+    smalls[1].wait()
+    smalls[2].wait()
     shards = iota((8, TILE), 1)
     first = shards * held
-
-    def reach(i, carry):
-        low, high, count, far = carry
-        spot = loc_ref[NOBS - 1 - i]
-        near = (spot >= low) & (spot <= high)
+    zeros = jnp.zeros((8, TILE), jnp.int32)
+    blank = jnp.zeros((1, TILE), jnp.int32)
+    index = iota((1, TILE), 1)
+    own_low = state * held - REACH
+    own_high = state * held + held + REACH
+
+    def relate(i, carry):
+        lows, highs, count, far, low, high, total, direct, spots, slots, obs, touch, vals, errs = carry
+        j = NOBS - 1 - i
+        spot = loc_ref[j]
+        near = (spot >= lows) & (spot <= highs)
         away = jnp.abs((spot >> 13) - (shards >> 1)) > WINDOW
         count = count + ((spot >> 12) == shards).astype(jnp.int32)
         far = jnp.where((near & away) | (count > SLOTS), 1, far)
-        low = jnp.where(near, jnp.minimum(low, spot - LINK), low)
-        high = jnp.where(near, jnp.maximum(high, spot + LINK), high)
-        return low, high, count, far
-
-    zeros = jnp.zeros((8, TILE), jnp.int32)
-    far = lax.fori_loop(
-        0, NOBS, reach, (first - REACH, first + held + REACH, zeros, zeros), unroll=8
-    )[3]
+        lows = jnp.where(near, jnp.minimum(lows, spot - LINK), lows)
+        highs = jnp.where(near, jnp.maximum(highs, spot + LINK), highs)
+        here = (spot >= low) & (spot <= high)
+        low = jnp.where(here, jnp.minimum(low, spot - LINK), low)
+        high = jnp.where(here, jnp.maximum(high, spot + LINK), high)
+        touches = (spot >= own_low) & (spot <= own_high)
+        slots = slots + ((spots >> 12) == (spot >> 12)).astype(jnp.int32)
+        place = index == jnp.where(here, total, -1)
+        spots = jnp.where(place, spot, spots)
+        slots = jnp.where(place, 0, slots)
+        obs = jnp.where(place, j, obs)
+        vals = jnp.where(place, val_ref[j], vals)
+        errs = jnp.where(place, err_ref[j], errs)
+        touch = jnp.where(index == jnp.where(touches, direct, -1), total, touch)
+        total = total + here.astype(jnp.int32)
+        direct = direct + touches.astype(jnp.int32)
+        return lows, highs, count, far, low, high, total, direct, spots, slots, obs, touch, vals, errs
+
+    nothing = jnp.zeros((1, TILE), jnp.float32)
+    related = lax.fori_loop(
+        0,
+        NOBS,
+        relate,
+        (
+            first - REACH, first + held + REACH, zeros, zeros, own_low, own_high,
+            jnp.int32(0), jnp.int32(0), blank - held, blank, blank, blank, nothing, nothing,
+        ),
+        unroll=4,
+    )
+    far, total, direct, spots, slots, obs, touch, vals, errs = (related[3],) + related[6:]
     far_ref[0, 0] = jnp.max(far)
+    base = (((spots >> 13) - chip + WINDOW) * CORES + ((spots >> 12) & 1)) * REPS
+    totals = jnp.where(index == 0, total, direct)
+    columns = (spots, base, slots * part_rows, obs, touch, totals)
+    for number, column in enumerate(columns):
+        table_ref[number : number + 1, :] = column.astype(jnp.float32)
+    table_ref[6:7, :] = vals
+    table_ref[7:8, :] = errs
+    outs = [
+        pltpu.make_async_copy(far_ref, far_out, small_sem.at[3]),
+        pltpu.make_async_copy(table_ref, table_out, small_sem.at[4]),
+    ]
+    for out in outs:
+        out.start()
 
     relays = []
     for step in range(half):
@@ -219,6 +276,9 @@
     for copy in to_right + to_left:
         copy.wait_send()
     pltpu.make_async_copy(nearby, nearby, near_send).wait()
+    block_copy.wait()
+    for out in outs:
+        out.wait()
 
     for n in shifts:
 
@@ -228,7 +288,7 @@
             pltpu.make_async_copy(block(n), block(n), row_recv.at[WINDOW + n]).wait()
 
 
-def gather(mesh, ensemble, locations):
+def gather(mesh, ensemble, locations, values, errors):
     part_rows, held = ensemble.shape
     dma = pltpu.SemaphoreType.DMA
     return pl.pallas_call(
@@ -236,15 +296,18 @@
         out_shape=(
             jax.ShapeDtypeStruct((ROWS, 1, TILE), jnp.float32),
             jax.ShapeDtypeStruct((REPS, part_rows, held), jnp.float32),
+            jax.ShapeDtypeStruct((8, TILE), jnp.float32),
             jax.ShapeDtypeStruct((1, 1), jnp.int32),
         ),
-        in_specs=[pl.BlockSpec(memory_space=pltpu.SMEM), pl.BlockSpec(memory_space=pl.ANY)],
-        out_specs=(
-            pl.BlockSpec(memory_space=pl.ANY),
-            pl.BlockSpec(memory_space=pl.ANY),
-            pl.BlockSpec(memory_space=pltpu.SMEM),
-        ),
+        in_specs=[pl.BlockSpec(memory_space=pl.ANY)] * 4,
+        out_specs=(pl.BlockSpec(memory_space=pl.ANY),) * 4,
         scratch_shapes=[
+            pltpu.SMEM((NOBS,), jnp.int32),
+            pltpu.SMEM((NOBS,), jnp.float32),
+            pltpu.SMEM((NOBS,), jnp.float32),
+            pltpu.SMEM((1, 1), jnp.int32),
+            pltpu.VMEM((8, TILE), jnp.float32),
+            dma((5,)), dma,
             pltpu.VMEM((part_rows, held), jnp.float32),
             pltpu.VMEM((held // TILE, part_rows, TILE), jnp.float32),
             pltpu.VMEM((1, 1, TILE), jnp.float32),
@@ -255,77 +318,37 @@
         ],
         compiler_params=pltpu.CompilerParams(collective_id=0, has_side_effects=True),
         name="gather",
-    )(locations, ensemble)
+    )(locations, values, errors, ensemble)
 
 
 def solve_kernel(
-    windowed, held, loc_ref, val_ref, err_ref, rows_ref, ens_ref, all_ref, out_ref,
-    s_ref, y_ref, u_ref, w_ref, center_ref, mutual_ref, tile_ref,
-    flag_ref, list_ref, slot_ref, direct_ref, count_ref, load_sem, out_sem,
+    windowed, held, table_ref, rows_ref, all_ref, out_ref,
+    y_ref, u_ref, w_ref, center_ref, mutual_ref, tile_ref,
 ):
     state = lax.axis_index("state")
     rep = lax.axis_index("rep")
-    chip = state // CORES
-    part_rows = ens_ref.shape[0]
-
-    def rows_of(index):
-        return pl.ds(pl.multiple_of(index * part_rows, part_rows), part_rows)
-
-    loads = [pltpu.make_async_copy(ens_ref, s_ref.at[rows_of(rep)], load_sem.at[0])]
-    for step in range(1, REPS):
-        other = (rep + step) % REPS
-        loads.append(
-            pltpu.make_async_copy(all_ref.at[other], s_ref.at[rows_of(other)], load_sem.at[step])
-        )
-    for load in loads:
-        load.start()
-
-    low_own = state * held - REACH
-    high_own = state * held + held + REACH
-
-    def mark(i, carry):
-        low, high = carry
-        j = NOBS - 1 - i
-        spot = loc_ref[j]
-        near = (spot >= low) & (spot <= high)
-        flag_ref[j] = near.astype(jnp.int32)
-        count_ref[spot // held] = 0
-        low = jnp.where(near, jnp.minimum(low, spot - LINK), low)
-        high = jnp.where(near, jnp.maximum(high, spot + LINK), high)
-        return low, high
-
-    lax.fori_loop(0, NOBS, mark, (low_own, high_own))
-
-    def enlist(j, carry):
-        total, direct = carry
-        spot = loc_ref[j]
-        shard = spot // held
-        rank = count_ref[shard]
-        count_ref[shard] = rank + 1
-        list_ref[total] = j
-        slot_ref[total] = rank
-        direct_ref[direct] = total
-        touches = (spot >= low_own) & (spot <= high_own)
-        return total + flag_ref[j], direct + touches.astype(jnp.int32)
-
-    total, direct = lax.fori_loop(0, NOBS, enlist, (jnp.int32(0), jnp.int32(0)))
-
+    part_rows = all_ref.shape[1]
+    order = [(rep + step) & (REPS - 1) for step in range(REPS)]
+
+    def entry(number, t):
+        return table_ref[number, t].astype(jnp.int32)
+
+    total = entry(5, 0)
+    direct = entry(5, 1)
     diagonal = iota((part_rows, TILE), 1) - iota((part_rows, TILE), 0)
 
     def spread(t, carry):
-        j = list_ref[t]
-        spot = loc_ref[j]
-        shard = spot // held
+        spot = entry(0, t)
         if windowed:
-            base = ((shard // CORES - chip + WINDOW) * CORES + shard % CORES) * REPS
-            place = slot_ref[t] * part_rows
+            base = entry(1, t)
+            place = entry(2, t)
         else:
-            base = j * REPS
+            base = entry(3, t) * REPS
             place = 0
-        for r in range(REPS):
-            row = jnp.broadcast_to(rows_ref[base + r], (part_rows, TILE))
+        for step in range(REPS):
+            row = jnp.broadcast_to(rows_ref[base + order[step]], (part_rows, TILE))
             column = jnp.sum(jnp.where(diagonal == place, row, 0.0), axis=1, keepdims=True)
-            y_ref[t, r * part_rows : (r + 1) * part_rows, :] = jnp.broadcast_to(
+            y_ref[t, step * part_rows : (step + 1) * part_rows, :] = jnp.broadcast_to(
                 column, (part_rows, TILE)
             )
         center = (spot // TILE * TILE).astype(jnp.float32) + (TILE - 1) * 0.5
@@ -339,10 +362,10 @@
         TILE - 1
     ) * 0.5
 
-    def assimilate(t, carry):
-        j = list_ref[t]
-        spot = loc_ref[j].astype(jnp.float32)
-        error = err_ref[j]
+    def assimilate(i, carry):
+        t = total - 1 - i
+        spot = table_ref[0, t]
+        error = table_ref[7, t]
         y = y_ref[t]
         mean = jnp.sum(y, axis=0, keepdims=True) * (1.0 / M)
         spread_of = y - mean
@@ -350,7 +373,7 @@
         total_var = variance + error
         shrink = 1.0 / (1.0 + jnp.sqrt(error / total_var))
         u = spread_of * (1.0 / ((M - 1) * total_var))
-        w = (val_ref[j] - mean) - shrink * spread_of
+        w = (table_ref[6, t] - mean) - shrink * spread_of
         u_ref[t] = u
         w_ref[t] = w
         mutual_ref[...] = taper(jnp.abs(center_ref[...] - spot))
@@ -362,13 +385,10 @@
             y_ref[k] = other + w * (mutual_ref[pl.ds(k, 1), :] * projected)
             return inner
 
-        lax.fori_loop(t + 1, total, update, 0)
+        lax.fori_loop(0, t, update, 0)
         return carry
 
     lax.fori_loop(0, total, assimilate, 0)
-
-    for load in loads:
-        load.wait()
     group = 4
 
     def apply(g, carry):
@@ -377,7 +397,7 @@
         ]
 
         def one(d, values):
-            t = direct_ref[d]
+            t = entry(4, direct - 1 - d)
             u = u_ref[t]
             w = w_ref[t]
             result = []
@@ -387,43 +407,34 @@
                 result.append(values[i] + w * (weight * projected))
             return tuple(result)
 
-        values = lax.fori_loop(0, direct, one, tuple(s_ref[:, span] for span in spans))
+        start = tuple(
+            jnp.concatenate([all_ref[member, :, span] for member in order], axis=0)
+            for span in spans
+        )
+        values = lax.fori_loop(0, direct, one, start)
         for span, value in zip(spans, values):
-            s_ref[:, span] = value
+            out_ref[:, span] = value[:part_rows]
         return carry
 
     lax.fori_loop(0, tiles // group, apply, 0)
-    store = pltpu.make_async_copy(s_ref.at[rows_of(rep)], out_ref, out_sem)
-    store.start()
-    store.wait()
-
-
-def solve(windowed, ensemble, values, errors, locations, rows, everything):
-    part_rows, held = ensemble.shape
-    smem = pl.BlockSpec(memory_space=pltpu.SMEM)
-    anywhere = pl.BlockSpec(memory_space=pl.ANY)
+
+
+def solve(windowed, part_rows, held, table, rows, everything):
+    vmem = pl.BlockSpec(memory_space=pltpu.VMEM)
     block = pltpu.VMEM((NOBS, M, TILE), jnp.float32)
     return pl.pallas_call(
         functools.partial(solve_kernel, windowed, held),
         out_shape=jax.ShapeDtypeStruct((part_rows, held), jnp.float32),
-        in_specs=[smem, smem, smem, pl.BlockSpec(memory_space=pltpu.VMEM), anywhere, anywhere],
-        out_specs=anywhere,
+        in_specs=[pl.BlockSpec(memory_space=pltpu.SMEM), vmem, vmem],
+        out_specs=vmem,
         scratch_shapes=[
-            pltpu.VMEM((M, held), jnp.float32),
             block, block, block,
             pltpu.VMEM((NOBS, TILE), jnp.float32),
             pltpu.VMEM((NOBS, TILE), jnp.float32),
             pltpu.VMEM((NOBS, held // TILE, TILE), jnp.float32),
-            pltpu.SMEM((NOBS,), jnp.int32),
-            pltpu.SMEM((NOBS,), jnp.int32),
-            pltpu.SMEM((NOBS,), jnp.int32),
-            pltpu.SMEM((NOBS,), jnp.int32),
-            pltpu.SMEM((128,), jnp.int32),
-            pltpu.SemaphoreType.DMA((REPS,)),
-            pltpu.SemaphoreType.DMA,
         ],
         name="solve",
-    )(locations, values, errors, rows, ensemble, everything)
+    )(table, rows, everything)
 
 
 def full_rows(mesh, ensemble, locations):
@@ -449,13 +460,13 @@
 
 
 def on_device(mesh, ensemble, obs_values, obs_error, obs_location):
-    rows, everything, far = gather(mesh, ensemble, obs_location)
+    part_rows, held = ensemble.shape
+    rows, everything, table, far = gather(mesh, ensemble, obs_location, obs_values, obs_error)
     return lax.cond(
         far[0, 0] == 0,
-        lambda: solve(True, ensemble, obs_values, obs_error, obs_location, rows, everything),
+        lambda: solve(True, part_rows, held, table, rows, everything),
         lambda: solve(
-            False, ensemble, obs_values, obs_error, obs_location,
-            full_rows(mesh, ensemble, obs_location), everything,
+            False, part_rows, held, table, full_rows(mesh, ensemble, obs_location), everything
         ),
     )
 

time: 29.1 us -> 24.7 us (0.85)
  the two profiles are of different devices: /device:TPU:6 before, /device:TPU:35 now
where the time goes in v4:
time: 24.7 us; the launch traced here: 24.6 us
  Pallas kernels  23.2 us (94%)
  local copies, waits for them, and re-layouts  0.7 us (3%)
  between operations  0.66 us (3%)
    pallas_call x1, Pallas kernels, gather(): pl.pallas_call(functools.partial(gather_kernel, mesh.shape['state'] // CO...  18.1 us
    pallas_call x1, Pallas kernels, solve(): pl.pallas_call(functools.partial(solve_kernel, windowed, held), out_shape...  5.18 us
    unnamed x2, local copies, waits for them, and re-layouts  0.7 us

profile of v4, /device:TPU:35, one launch (start us, length us, event | category | flops | bytes accessed | tf_op | source)
XLA Modules:
  0.0 24.6 jit_solution(2413796443258575702)
XLA Ops:
  0.0 18.1 %gather.9 = (f32[72,1,128]{2,1,0:T(1,128)S(1)}, f32[4,16,4096]{2,1,0:T(8,128)S(1)}, f32[8,128]{1,0:T(8,128)S(1)}, s32[1,1]{1,0:T(1,128)}) custom-call(s32[48]{0:T(128)} %loc_any.1, f32[48]{0:T(128)} %val_any.1, f32[48]{0:T(128)} %err_any.1, f32[16,4096]{1,0:T(8,128)} %ens_ref.1), custom_call_target="tpu_custom_call" | custom-call | tf_op jit(solution)/shard_map/gather/pallas_call | solution.py:294
  18.7 5.2 %conditional.1 = (f32[16,4096]{1,0:T(8,128)S(1)}) conditional(s32[]{:T(128)} %bitcast.5, (s32[48]{0:T(128)}, f32[16,4096]{1,0:T(8,128)}, f32[8,128]{1,0:T(8,128)S(1)}, f32[4,16,4096]{2,1,0:T(8,128)S(1)}) %tuple.11, (f32[8,128]{1,0:T(8,128)S(1)}, f32[72,1,128]{2,1,0:T(1,128)S(1)}, f32[4,16,4096]{2,1,0:T(8,128)S(1)}) %tuple.12), branch_computations={%region_0.1_spmd, %region_1.2_spmd} | conditional | flops 30025 | bytes 1545686 | solution.py:465
  18.7 5.2 %solve.3 = f32[16,4096]{1,0:T(8,128)S(1)} custom-call(f32[8,128]{1,0:T(8,128)S(1)} %get-tuple-element.26.table_ref, f32[72,1,128]{2,1,0:T(1,128)S(1)} %get-tuple-element.27.rows_ref, f32[4,16,4096]{2,1,0:T(8,128)S(1)} %get-tuple-element.28.all_ref), custom_call_target="tpu_custom_call" | custom-call | tf_op jit(solution)/shard_map/cond/branch_1_fun/solve/pallas_call | solution.py:425
  23.9 0.0 copy-start
  23.9 0.7 %copy-done = f32[16,4096]{1,0:T(8,128)} copy-done((f32[16,4096]{1,0:T(8,128)}, f32[16,4096]{1,0:T(8,128)S(1)}, u32[]{:S(2)}) %copy-start) | copy-done | bytes 262168
Async XLA Ops:
  23.9 0.7 %copy-start = (f32[16,4096]{1,0:T(8,128)}, f32[16,4096]{1,0:T(8,128)S(1)}, u32[]{:S(2)}) copy-start(f32[16,4096]{1,0:T(8,128)S(1)} %get-tuple-element.54) | copy-start | bytes 786436

commit v5 on v4

--- a/solution.py
+++ b/solution.py
@@ -90,7 +90,33 @@
     def count_of(flags):
         return sum(flags[n].astype(jnp.int32) for n in shifts)
 
+    right = (state, reps_of[1])
+    left = (state, reps_of[3])
+    width = held // CHUNKS
+
+    def piece(ref, chunk):
+        return ref.at[:, pl.ds(chunk * width, width)]
+
+    def bulk(source, owner, chunk, target, send_sem, recv_sem):
+        return pltpu.make_async_remote_copy(
+            src_ref=piece(source, chunk),
+            dst_ref=piece(all_ref.at[owner], chunk),
+            send_sem=send_sem.at[chunk],
+            recv_sem=recv_sem.at[chunk],
+            device_id=target,
+            device_id_type=MESH,
+        )
+
+    half = CHUNKS // 2
+    to_right = [bulk(ens_ref, rep, c, right, send_right, recv_left) for c in range(CHUNKS)]
+    to_left = [bulk(ens_ref, rep, c, left, send_left, recv_right) for c in range(CHUNKS)]
     barrier = pltpu.get_barrier_semaphore()
+    wraps = {n: valid[n] & (((chip + n) & ~(DEPTH - 1)) != (chip & ~(DEPTH - 1))) for n in shifts}
+    greetings = (
+        len(beside)
+        + count_of(earlier)
+        + (len(members) - 1) * count_of({n: earlier[n] & wraps[n] for n in shifts})
+    )
     for member in beside:
         signal(barrier, 0, member)
     for n in shifts:
@@ -98,6 +124,13 @@
         @pl.when(later[n])
         def _(n=n):
             signal(barrier, n, members[0])
+
+    for n in shifts:
+
+        @pl.when(later[n] & wraps[n])
+        def _(n=n):
+            for member in beside:
+                signal(barrier, n, member)
 
     smalls[0].wait()
     load.wait()
@@ -121,7 +154,25 @@
         rank = rank + inside.astype(jnp.int32)
     pick_ref[0] = jnp.sum(packed, axis=0, keepdims=True)
 
-    pl.semaphore_wait(barrier, len(beside) + count_of(earlier))
+    pl.semaphore_wait(barrier, greetings)
+
+    def send_row(shift, member):
+        slot = ((WINDOW - shift) * CORES + core) * REPS + rep
+        pltpu.make_async_remote_copy(
+            src_ref=pick_ref.at[0],
+            dst_ref=rows_ref.at[slot],
+            send_sem=row_send.at[WINDOW + shift],
+            recv_sem=row_recv.at[WINDOW - shift],
+            device_id=target(shift, member),
+            device_id_type=MESH,
+        ).start()
+
+    for n in range(WINDOW, 0, -1):
+
+        @pl.when(earlier[n] & wraps[n])
+        def _(n=n):
+            for member in members:
+                send_row(n, member)
 
     own_row = (WINDOW * CORES + core) * REPS + rep
     for member in beside:
@@ -154,26 +205,6 @@
             device_id_type=MESH,
         ).start()
 
-    right = (state, reps_of[1])
-    left = (state, reps_of[3])
-    width = held // CHUNKS
-
-    def piece(ref, chunk):
-        return ref.at[:, pl.ds(chunk * width, width)]
-
-    def bulk(source, owner, chunk, target, send_sem, recv_sem):
-        return pltpu.make_async_remote_copy(
-            src_ref=piece(source, chunk),
-            dst_ref=piece(all_ref.at[owner], chunk),
-            send_sem=send_sem.at[chunk],
-            recv_sem=recv_sem.at[chunk],
-            device_id=target,
-            device_id_type=MESH,
-        )
-
-    half = CHUNKS // 2
-    to_right = [bulk(ens_ref, rep, c, right, send_right, recv_left) for c in range(CHUNKS)]
-    to_left = [bulk(ens_ref, rep, c, left, send_left, recv_right) for c in range(CHUNKS)]
     for step in range(CHUNKS):
         to_right[step].start()
         to_left[(step + half) % CHUNKS].start()
@@ -183,7 +214,7 @@
     pltpu.make_async_copy(nearby, nearby, near_recv).wait()
     for n in shifts:
 
-        @pl.when(earlier[n])
+        @pl.when(earlier[n] & jnp.logical_not(wraps[n]))
         def _(n=n):
             send_block(n)
 

time: 24.7 us -> 25.4 us (1.028)
  the two profiles are of different devices: /device:TPU:35 before, /device:TPU:1 now
where the time goes in v5:
time: 25.4 us; the launch traced here: 25.2 us
  Pallas kernels  23.9 us (94%)
  local copies, waits for them, and re-layouts  0.7 us (3%)
  between operations  0.66 us (3%)
    pallas_call x1, Pallas kernels, gather(): pl.pallas_call(functools.partial(gather_kernel, mesh.shape['state'] // CO...  20.5 us
    pallas_call x1, Pallas kernels, solve(): pl.pallas_call(functools.partial(solve_kernel, windowed, held), out_shape...  3.39 us
    unnamed x2, local copies, waits for them, and re-layouts  0.7 us

profile of v5, /device:TPU:1, one launch (start us, length us, event | category | flops | bytes accessed | tf_op | source)
XLA Modules:
  0.0 25.2 jit_solution(17526134432955016716)
XLA Ops:
  0.0 20.5 %gather.9 = (f32[72,1,128]{2,1,0:T(1,128)S(1)}, f32[4,16,4096]{2,1,0:T(8,128)S(1)}, f32[8,128]{1,0:T(8,128)S(1)}, s32[1,1]{1,0:T(1,128)}) custom-call(s32[48]{0:T(128)} %loc_any.1, f32[48]{0:T(128)} %val_any.1, f32[48]{0:T(128)} %err_any.1, f32[16,4096]{1,0:T(8,128)} %ens_ref.1), custom_call_target="tpu_custom_call" | custom-call | tf_op jit(solution)/shard_map/gather/pallas_call | solution.py:325
  21.1 3.4 %conditional.1 = (f32[16,4096]{1,0:T(8,128)S(1)}) conditional(s32[]{:T(128)} %bitcast.5, (s32[48]{0:T(128)}, f32[16,4096]{1,0:T(8,128)}, f32[8,128]{1,0:T(8,128)S(1)}, f32[4,16,4096]{2,1,0:T(8,128)S(1)}) %tuple.11, (f32[8,128]{1,0:T(8,128)S(1)}, f32[72,1,128]{2,1,0:T(1,128)S(1)}, f32[4,16,4096]{2,1,0:T(8,128)S(1)}) %tuple.12), branch_computations={%region_0.1_spmd, %region_1.2_spmd} | conditional | flops 30025 | bytes 1545686 | solution.py:496
  21.1 3.4 %solve.3 = f32[16,4096]{1,0:T(8,128)S(1)} custom-call(f32[8,128]{1,0:T(8,128)S(1)} %get-tuple-element.26.table_ref, f32[72,1,128]{2,1,0:T(1,128)S(1)} %get-tuple-element.27.rows_ref, f32[4,16,4096]{2,1,0:T(8,128)S(1)} %get-tuple-element.28.all_ref), custom_call_target="tpu_custom_call" | custom-call | tf_op jit(solution)/shard_map/cond/branch_1_fun/solve/pallas_call | solution.py:456
  24.5 0.0 copy-start
  24.5 0.7 %copy-done = f32[16,4096]{1,0:T(8,128)} copy-done((f32[16,4096]{1,0:T(8,128)}, f32[16,4096]{1,0:T(8,128)S(1)}, u32[]{:S(2)}) %copy-start) | copy-done | bytes 262168
Async XLA Ops:
  24.5 0.7 %copy-start = (f32[16,4096]{1,0:T(8,128)}, f32[16,4096]{1,0:T(8,128)S(1)}, u32[]{:S(2)}) copy-start(f32[16,4096]{1,0:T(8,128)S(1)} %get-tuple-element.54) | copy-start | bytes 786436

commit v6 on v5

--- a/solution.py
+++ b/solution.py
@@ -76,6 +76,8 @@
     earlier = {n: valid[n] & jnp.logical_not(ahead[n]) for n in shifts}
     members = [(c, r) for c in range(CORES) for r in range(REPS)]
     beside = members[1:]
+    peers = members[1:REPS]
+    pair = members[REPS]
     cores_of = [core, 1 - core]
     reps_of = [(rep + r) & (REPS - 1) for r in range(REPS)]
 
@@ -113,12 +115,18 @@
     barrier = pltpu.get_barrier_semaphore()
     wraps = {n: valid[n] & (((chip + n) & ~(DEPTH - 1)) != (chip & ~(DEPTH - 1))) for n in shifts}
     greetings = (
-        len(beside)
+        len(peers)
+        + (1 - core)
         + count_of(earlier)
         + (len(members) - 1) * count_of({n: earlier[n] & wraps[n] for n in shifts})
     )
-    for member in beside:
+    for member in peers:
         signal(barrier, 0, member)
+
+    @pl.when(core == 1)
+    def _():
+        signal(barrier, 0, pair)
+
     for n in shifts:
 
         @pl.when(later[n])
@@ -175,7 +183,7 @@
                 send_row(n, member)
 
     own_row = (WINDOW * CORES + core) * REPS + rep
-    for member in beside:
+    for member in peers:
         pltpu.make_async_remote_copy(
             src_ref=pick_ref.at[0],
             dst_ref=rows_ref.at[own_row],
@@ -186,6 +194,11 @@
         ).start()
     own = pltpu.make_async_copy(pick_ref.at[0], rows_ref.at[own_row], own_sem)
     own.start()
+
+    @pl.when(core == 0)
+    def _():
+        signal(late_sem.at[WINDOW], 0, pair)
+
     for n in shifts:
 
         @pl.when(earlier[n])
@@ -209,9 +222,25 @@
         to_right[step].start()
         to_left[(step + half) % CHUNKS].start()
 
+    half_block = rows_ref.at[pl.ds(WINDOW * len(members) + core * REPS, REPS)]
+    to_pair = pltpu.make_async_remote_copy(
+        src_ref=half_block,
+        dst_ref=half_block,
+        send_sem=row_send.at[WINDOW],
+        recv_sem=row_recv.at[WINDOW],
+        device_id=target(0, pair),
+        device_id_type=MESH,
+    )
     own.wait()
-    nearby = block(0, len(beside))
+    nearby = block(0, len(peers))
     pltpu.make_async_copy(nearby, nearby, near_recv).wait()
+
+    @pl.when(core == 1)
+    def _():
+        pl.semaphore_wait(late_sem.at[WINDOW], 1)
+
+    to_pair.start()
+    to_pair.wait_recv()
     for n in shifts:
 
         @pl.when(earlier[n] & jnp.logical_not(wraps[n]))
@@ -307,6 +336,7 @@
     for copy in to_right + to_left:
         copy.wait_send()
     pltpu.make_async_copy(nearby, nearby, near_send).wait()
+    to_pair.wait_send()
     block_copy.wait()
     for out in outs:
         out.wait()

time: 25.4 us -> 23.6 us (0.929)
  the two profiles are of different devices: /device:TPU:1 before, /device:TPU:135 now
where the time goes in v6:
time: 23.6 us; the launch traced here: 23.5 us
  Pallas kernels  22.1 us (94%)
  local copies, waits for them, and re-layouts  0.7 us (3%)
  between operations  0.66 us (3%)
    pallas_call x1, Pallas kernels, gather(): pl.pallas_call(functools.partial(gather_kernel, mesh.shape['state'] // CO...  18.2 us
    pallas_call x1, Pallas kernels, solve(): pl.pallas_call(functools.partial(solve_kernel, windowed, held), out_shape...  3.93 us
    unnamed x2, local copies, waits for them, and re-layouts  0.7 us

profile of v6, /device:TPU:135, one launch (start us, length us, event | category | flops | bytes accessed | tf_op | source)
XLA Modules:
  0.0 23.5 jit_solution(12338762000782894664)
XLA Ops:
  0.0 18.2 %gather.9 = (f32[72,1,128]{2,1,0:T(1,128)S(1)}, f32[4,16,4096]{2,1,0:T(8,128)S(1)}, f32[8,128]{1,0:T(8,128)S(1)}, s32[1,1]{1,0:T(1,128)}) custom-call(s32[48]{0:T(128)} %loc_any.1, f32[48]{0:T(128)} %val_any.1, f32[48]{0:T(128)} %err_any.1, f32[16,4096]{1,0:T(8,128)} %ens_ref.1), custom_call_target="tpu_custom_call" | custom-call | tf_op jit(solution)/shard_map/gather/pallas_call | solution.py:355
  18.8 4.0 %conditional.1 = (f32[16,4096]{1,0:T(8,128)S(1)}) conditional(s32[]{:T(128)} %bitcast.5, (s32[48]{0:T(128)}, f32[16,4096]{1,0:T(8,128)}, f32[8,128]{1,0:T(8,128)S(1)}, f32[4,16,4096]{2,1,0:T(8,128)S(1)}) %tuple.11, (f32[8,128]{1,0:T(8,128)S(1)}, f32[72,1,128]{2,1,0:T(1,128)S(1)}, f32[4,16,4096]{2,1,0:T(8,128)S(1)}) %tuple.12), branch_computations={%region_0.1_spmd, %region_1.2_spmd} | conditional | flops 30025 | bytes 1545686 | solution.py:526
  18.8 3.9 %solve.3 = f32[16,4096]{1,0:T(8,128)S(1)} custom-call(f32[8,128]{1,0:T(8,128)S(1)} %get-tuple-element.26.table_ref, f32[72,1,128]{2,1,0:T(1,128)S(1)} %get-tuple-element.27.rows_ref, f32[4,16,4096]{2,1,0:T(8,128)S(1)} %get-tuple-element.28.all_ref), custom_call_target="tpu_custom_call" | custom-call | tf_op jit(solution)/shard_map/cond/branch_1_fun/solve/pallas_call | solution.py:486
  22.8 0.0 copy-start
  22.8 0.7 %copy-done = f32[16,4096]{1,0:T(8,128)} copy-done((f32[16,4096]{1,0:T(8,128)}, f32[16,4096]{1,0:T(8,128)S(1)}, u32[]{:S(2)}) %copy-start) | copy-done | bytes 262168
Async XLA Ops:
  22.8 0.7 %copy-start = (f32[16,4096]{1,0:T(8,128)}, f32[16,4096]{1,0:T(8,128)S(1)}, u32[]{:S(2)}) copy-start(f32[16,4096]{1,0:T(8,128)S(1)} %get-tuple-element.54) | copy-start | bytes 786436

commit v7 on v6

--- a/solution.py
+++ b/solution.py
@@ -20,6 +20,7 @@
 DEPTH = 16
 SLOTS = 8
 CHUNKS = 4
+BATCH = 4
 ROWS = (2 * WINDOW + 1) * CORES * REPS
 
 
@@ -384,7 +385,7 @@
 
 def solve_kernel(
     windowed, held, table_ref, rows_ref, all_ref, out_ref,
-    y_ref, u_ref, w_ref, center_ref, mutual_ref, tile_ref,
+    y_ref, u_ref, w_ref, center_ref, mutual_ref, tile_ref, done_ref, out_sem,
 ):
     state = lax.axis_index("state")
     rep = lax.axis_index("rep")
@@ -398,10 +399,10 @@
     direct = entry(5, 1)
     diagonal = iota((part_rows, TILE), 1) - iota((part_rows, TILE), 0)
 
-    def spread(t, carry):
+    def spread(t):
         spot = entry(0, t)
         if windowed:
-            base = entry(1, t)
+            base = jnp.clip(entry(1, t), 0, ROWS - REPS)
             place = entry(2, t)
         else:
             base = entry(3, t) * REPS
@@ -412,11 +413,18 @@
             y_ref[t, step * part_rows : (step + 1) * part_rows, :] = jnp.broadcast_to(
                 column, (part_rows, TILE)
             )
-        center = (spot // TILE * TILE).astype(jnp.float32) + (TILE - 1) * 0.5
+        center = ((spot >> 7) << 7).astype(jnp.float32) + (TILE - 1) * 0.5
         center_ref[pl.ds(t, 1), :] = jnp.full((1, TILE), center, jnp.float32)
+
+    def spread_batch(b, carry):
+        for i in range(BATCH):
+            spread(b * BATCH + i)
         return carry
 
-    lax.fori_loop(0, total, spread, 0)
+    def batches(number):
+        return (number + BATCH - 1) // BATCH
+
+    lax.fori_loop(0, batches(total), spread_batch, 0)
 
     tiles = held // TILE
     tile_centers = (state * held + iota((tiles, TILE), 0) * TILE).astype(jnp.float32) + (
@@ -440,13 +448,17 @@
         mutual_ref[...] = taper(jnp.abs(center_ref[...] - spot))
         tile_ref[t] = taper(jnp.abs(tile_centers - spot))
 
-        def update(k, inner):
-            other = y_ref[k]
-            projected = jnp.sum(u * other, axis=0, keepdims=True)
-            y_ref[k] = other + w * (mutual_ref[pl.ds(k, 1), :] * projected)
+        def update(b, inner):
+            first = b * BATCH
+            others = [y_ref[first + i] for i in range(BATCH)]
+            for i, other in enumerate(others):
+                projected = jnp.sum(u * other, axis=0, keepdims=True)
+                others[i] = other + w * (mutual_ref[pl.ds(first + i, 1), :] * projected)
+            for i, other in enumerate(others):
+                y_ref[first + i] = other
             return inner
 
-        lax.fori_loop(0, t, update, 0)
+        lax.fori_loop(0, batches(t), update, 0)
         return carry
 
     lax.fori_loop(0, total, assimilate, 0)
@@ -474,10 +486,14 @@
         )
         values = lax.fori_loop(0, direct, one, start)
         for span, value in zip(spans, values):
-            out_ref[:, span] = value[:part_rows]
+            done_ref[:, span] = value[:part_rows]
+        width = group * TILE
+        wide = pl.ds(pl.multiple_of(g * width, width), width)
+        pltpu.make_async_copy(done_ref.at[:, wide], out_ref.at[:, wide], out_sem).start()
         return carry
 
     lax.fori_loop(0, tiles // group, apply, 0)
+    pltpu.make_async_copy(done_ref, out_ref, out_sem).wait()
 
 
 def solve(windowed, part_rows, held, table, rows, everything):
@@ -487,12 +503,15 @@
         functools.partial(solve_kernel, windowed, held),
         out_shape=jax.ShapeDtypeStruct((part_rows, held), jnp.float32),
         in_specs=[pl.BlockSpec(memory_space=pltpu.SMEM), vmem, vmem],
-        out_specs=vmem,
+        out_specs=pl.BlockSpec(memory_space=pl.ANY),
+        compiler_params=pltpu.CompilerParams(vmem_limit_bytes=65918864),
         scratch_shapes=[
             block, block, block,
             pltpu.VMEM((NOBS, TILE), jnp.float32),
             pltpu.VMEM((NOBS, TILE), jnp.float32),
             pltpu.VMEM((NOBS, held // TILE, TILE), jnp.float32),
+            pltpu.VMEM((part_rows, held), jnp.float32),
+            pltpu.SemaphoreType.DMA,
         ],
         name="solve",
     )(table, rows, everything)
@@ -523,11 +542,13 @@
 def on_device(mesh, ensemble, obs_values, obs_error, obs_location):
     part_rows, held = ensemble.shape
     rows, everything, table, far = gather(mesh, ensemble, obs_location, obs_values, obs_error)
-    return lax.cond(
-        far[0, 0] == 0,
-        lambda: solve(True, part_rows, held, table, rows, everything),
-        lambda: solve(
-            False, part_rows, held, table, full_rows(mesh, ensemble, obs_location), everything
+    return lax.switch(
+        far[0, 0],
+        (
+            lambda: solve(True, part_rows, held, table, rows, everything),
+            lambda: solve(
+                False, part_rows, held, table, full_rows(mesh, ensemble, obs_location), everything
+            ),
         ),
     )
 

time: 23.6 us -> 21.7 us (0.919)
  the two profiles are of different devices: /device:TPU:135 before, /device:TPU:1 now
where the time goes in v7:
time: 21.7 us; the launch traced here: 21.5 us
  Pallas kernels  21 us (97%)
  between operations  0.57 us (3%)
    pallas_call x1, Pallas kernels, gather(): pl.pallas_call(functools.partial(gather_kernel, mesh.shape['state'] // CO...  19 us
    pallas_call x1, Pallas kernels, solve(): pl.pallas_call(functools.partial(solve_kernel, windowed, held), out_shape...  2 us

profile of v7, /device:TPU:1, one launch (start us, length us, event | category | flops | bytes accessed | tf_op | source)
XLA Modules:
  0.0 21.5 jit_solution(15401145058047183829)
XLA Ops:
  0.0 19.0 %gather.9 = (f32[72,1,128]{2,1,0:T(1,128)S(1)}, f32[4,16,4096]{2,1,0:T(8,128)S(1)}, f32[8,128]{1,0:T(8,128)S(1)}, s32[1,1]{1,0:T(1,128)}) custom-call(s32[48]{0:T(128)} %loc_any.1, f32[48]{0:T(128)} %val_any.1, f32[48]{0:T(128)} %err_any.1, f32[16,4096]{1,0:T(8,128)} %ens_ref.1), custom_call_target="tpu_custom_call" | custom-call | tf_op jit(solution)/shard_map/gather/pallas_call | solution.py:356
  19.5 2.0 %conditional.1 = (f32[16,4096]{1,0:T(8,128)}) conditional(s32[]{:T(128)} %bitcast.5, (f32[8,128]{1,0:T(8,128)S(1)}, f32[72,1,128]{2,1,0:T(1,128)S(1)}, f32[4,16,4096]{2,1,0:T(8,128)S(1)}) %tuple.11, (s32[48]{0:T(128)}, f32[16,4096]{1,0:T(8,128)}, f32[8,128]{1,0:T(8,128)S(1)}, f32[4,16,4096]{2,1,0:T(8,128)S(1)}) %tuple.12), branch_computations={%region_0.0_spmd, %region_1.2_spmd} | conditional | flops 30025 | bytes 1545686 | solution.py:545
  19.5 2.0 %solve.2 = f32[16,4096]{1,0:T(8,128)} custom-call(f32[8,128]{1,0:T(8,128)S(1)} %get-tuple-element.22.table_ref, f32[72,1,128]{2,1,0:T(1,128)S(1)} %get-tuple-element.23.rows_ref, f32[4,16,4096]{2,1,0:T(8,128)S(1)} %get-tuple-element.24.all_ref), custom_call_target="tpu_custom_call" | custom-call | tf_op jit(solution)/shard_map/cond/branch_0_fun/solve/pallas_call | solution.py:502

commit v8 on v7

--- a/solution.py
+++ b/solution.py
@@ -114,12 +114,19 @@
     to_right = [bulk(ens_ref, rep, c, right, send_right, recv_left) for c in range(CHUNKS)]
     to_left = [bulk(ens_ref, rep, c, left, send_left, recv_right) for c in range(CHUNKS)]
     barrier = pltpu.get_barrier_semaphore()
-    wraps = {n: valid[n] & (((chip + n) & ~(DEPTH - 1)) != (chip & ~(DEPTH - 1))) for n in shifts}
+
+    def straight(n):
+        other = depth + n
+        apart = (chip + n) ^ chip
+        low = (depth > 0) & (other > 0) & (depth < DEPTH // 2) & (other < DEPTH // 2)
+        return valid[n] & (((apart & (DEPTH // 2)) != 0) | (low & ((apart & WINDOW) != 0)))
+
+    crosses = {n: straight(n) for n in shifts}
     greetings = (
         len(peers)
         + (1 - core)
         + count_of(earlier)
-        + (len(members) - 1) * count_of({n: earlier[n] & wraps[n] for n in shifts})
+        + (len(members) - 1) * count_of({n: earlier[n] & crosses[n] for n in shifts})
     )
     for member in peers:
         signal(barrier, 0, member)
@@ -136,7 +143,7 @@
 
     for n in shifts:
 
-        @pl.when(later[n] & wraps[n])
+        @pl.when(later[n] & crosses[n])
         def _(n=n):
             for member in beside:
                 signal(barrier, n, member)
@@ -176,9 +183,9 @@
             device_id_type=MESH,
         ).start()
 
-    for n in range(WINDOW, 0, -1):
-
-        @pl.when(earlier[n] & wraps[n])
+    for n in sorted(shifts, key=abs, reverse=True):
+
+        @pl.when(earlier[n] & crosses[n])
         def _(n=n):
             for member in members:
                 send_row(n, member)
@@ -244,9 +251,20 @@
     to_pair.wait_recv()
     for n in shifts:
 
-        @pl.when(earlier[n] & jnp.logical_not(wraps[n]))
+        @pl.when(earlier[n] & jnp.logical_not(crosses[n]))
         def _(n=n):
             send_block(n)
+
+    relays = []
+    for step in range(half):
+        to_right[step].wait_recv()
+        relay = bulk(all_ref.at[left[1]], left[1], step, right, pass_right, far_left)
+        relay.start()
+        relays.append(relay)
+        to_left[half + step].wait_recv()
+        relay = bulk(all_ref.at[right[1]], right[1], half + step, left, pass_left, far_right)
+        relay.start()
+        relays.append(relay)
 
     smalls[1].wait()
     smalls[2].wait()
@@ -310,17 +328,6 @@
     ]
     for out in outs:
         out.start()
-
-    relays = []
-    for step in range(half):
-        to_right[step].wait_recv()
-        relay = bulk(all_ref.at[left[1]], left[1], step, right, pass_right, far_left)
-        relay.start()
-        relays.append(relay)
-        to_left[half + step].wait_recv()
-        relay = bulk(all_ref.at[right[1]], right[1], half + step, left, pass_left, far_right)
-        relay.start()
-        relays.append(relay)
 
     for n in shifts:
 

time: 21.7 us -> 22 us (1.014); the launches traced: 21.5 us -> 22.1 us
  Pallas kernels: 21 us -> 21.5 us
    pallas_call x1, Pallas kernels: 2 us -> 2.83 us  [solve(): pl.pallas_call(functools.partial(solve_kernel, windowed, held), out_shape...]
    pallas_call x1, Pallas kernels: 19 us -> 18.7 us  [gather(): pl.pallas_call(functools.partial(gather_kernel, mesh.shape['state'] // CO...]
where the time goes in v8:
time: 22 us; the launch traced here: 22.1 us
  Pallas kernels  21.5 us (98%)
  between operations  0.57 us (3%)
    pallas_call x1, Pallas kernels, gather(): pl.pallas_call(functools.partial(gather_kernel, mesh.shape['state'] // CO...  18.7 us
    pallas_call x1, Pallas kernels, solve(): pl.pallas_call(functools.partial(solve_kernel, windowed, held), out_shape...  2.83 us

profile of v8, /device:TPU:1, one launch (start us, length us, event | category | flops | bytes accessed | tf_op | source)
XLA Modules:
  0.0 22.1 jit_solution(13748792773965006859)
XLA Ops:
  0.0 18.7 %gather.9 = (f32[72,1,128]{2,1,0:T(1,128)S(1)}, f32[4,16,4096]{2,1,0:T(8,128)S(1)}, f32[8,128]{1,0:T(8,128)S(1)}, s32[1,1]{1,0:T(1,128)}) custom-call(s32[48]{0:T(128)} %loc_any.1, f32[48]{0:T(128)} %val_any.1, f32[48]{0:T(128)} %err_any.1, f32[16,4096]{1,0:T(8,128)} %ens_ref.1), custom_call_target="tpu_custom_call" | custom-call | tf_op jit(solution)/shard_map/gather/pallas_call | solution.py:363
  19.2 2.9 %conditional.1 = (f32[16,4096]{1,0:T(8,128)}) conditional(s32[]{:T(128)} %bitcast.5, (f32[8,128]{1,0:T(8,128)S(1)}, f32[72,1,128]{2,1,0:T(1,128)S(1)}, f32[4,16,4096]{2,1,0:T(8,128)S(1)}) %tuple.11, (s32[48]{0:T(128)}, f32[16,4096]{1,0:T(8,128)}, f32[8,128]{1,0:T(8,128)S(1)}, f32[4,16,4096]{2,1,0:T(8,128)S(1)}) %tuple.12), branch_computations={%region_0.0_spmd, %region_1.2_spmd} | conditional | flops 30025 | bytes 1545686 | solution.py:552
  19.2 2.8 %solve.2 = f32[16,4096]{1,0:T(8,128)} custom-call(f32[8,128]{1,0:T(8,128)S(1)} %get-tuple-element.22.table_ref, f32[72,1,128]{2,1,0:T(1,128)S(1)} %get-tuple-element.23.rows_ref, f32[4,16,4096]{2,1,0:T(8,128)S(1)} %get-tuple-element.24.all_ref), custom_call_target="tpu_custom_call" | custom-call | tf_op jit(solution)/shard_map/cond/branch_0_fun/solve/pallas_call | solution.py:509

commit v9 on v8

--- a/solution.py
+++ b/solution.py
@@ -469,7 +469,7 @@
         return carry
 
     lax.fori_loop(0, total, assimilate, 0)
-    group = 4
+    group = 8
 
     def apply(g, carry):
         spans = [

time: 22 us -> 22.5 us (1.023); the launches traced: 22.1 us -> 22.3 us
    pallas_call x1, Pallas kernels: 2.83 us -> 3.09 us  [solve(): pl.pallas_call(functools.partial(solve_kernel, windowed, held), out_shape...]
where the time goes in v9:
time: 22.5 us; the launch traced here: 22.3 us
  Pallas kernels  21.7 us (96%)
  between operations  0.57 us (3%)
    pallas_call x1, Pallas kernels, gather(): pl.pallas_call(functools.partial(gather_kernel, mesh.shape['state'] // CO...  18.7 us
    pallas_call x1, Pallas kernels, solve(): pl.pallas_call(functools.partial(solve_kernel, windowed, held), out_shape...  3.09 us

profile of v9, /device:TPU:1, one launch (start us, length us, event | category | flops | bytes accessed | tf_op | source)
XLA Modules:
  0.0 22.3 jit_solution(10827974567053103220)
XLA Ops:
  0.0 18.7 %gather.9 = (f32[72,1,128]{2,1,0:T(1,128)S(1)}, f32[4,16,4096]{2,1,0:T(8,128)S(1)}, f32[8,128]{1,0:T(8,128)S(1)}, s32[1,1]{1,0:T(1,128)}) custom-call(s32[48]{0:T(128)} %loc_any.1, f32[48]{0:T(128)} %val_any.1, f32[48]{0:T(128)} %err_any.1, f32[16,4096]{1,0:T(8,128)} %ens_ref.1), custom_call_target="tpu_custom_call" | custom-call | tf_op jit(solution)/shard_map/gather/pallas_call | solution.py:363
  19.2 3.1 %conditional.1 = (f32[16,4096]{1,0:T(8,128)}) conditional(s32[]{:T(128)} %bitcast.5, (f32[8,128]{1,0:T(8,128)S(1)}, f32[72,1,128]{2,1,0:T(1,128)S(1)}, f32[4,16,4096]{2,1,0:T(8,128)S(1)}) %tuple.11, (s32[48]{0:T(128)}, f32[16,4096]{1,0:T(8,128)}, f32[8,128]{1,0:T(8,128)S(1)}, f32[4,16,4096]{2,1,0:T(8,128)S(1)}) %tuple.12), branch_computations={%region_0.0_spmd, %region_1.2_spmd} | conditional | flops 30025 | bytes 1545686 | solution.py:552
  19.2 3.1 %solve.2 = f32[16,4096]{1,0:T(8,128)} custom-call(f32[8,128]{1,0:T(8,128)S(1)} %get-tuple-element.22.table_ref, f32[72,1,128]{2,1,0:T(1,128)S(1)} %get-tuple-element.23.rows_ref, f32[4,16,4096]{2,1,0:T(8,128)S(1)} %get-tuple-element.24.all_ref), custom_call_target="tpu_custom_call" | custom-call | tf_op jit(solution)/shard_map/cond/branch_0_fun/solve/pallas_call | solution.py:509

commit v10 on v8

--- a/solution.py
+++ b/solution.py
@@ -55,6 +55,76 @@
     part_rows = ens_ref.shape[0]
     tiles = held // TILE
 
+    depth = chip & (DEPTH - 1)
+    shifts = list(range(1, WINDOW + 1)) + list(range(-1, -WINDOW - 1, -1))
+    valid = {n: (chip + n >= 0) & (chip + n < chips) for n in shifts}
+
+    def key(place):
+        return place + jnp.where((place >> 2) == 2, DEPTH, 0)
+
+    ahead = {n: key((depth + n) & (DEPTH - 1)) > key(depth) for n in shifts}
+    later = {n: valid[n] & ahead[n] for n in shifts}
+    earlier = {n: valid[n] & jnp.logical_not(ahead[n]) for n in shifts}
+    members = [(c, r) for c in range(CORES) for r in range(REPS)]
+    beside = members[1:]
+    peers = members[1:REPS]
+    pair = members[REPS]
+    cores_of = [core, 1 - core]
+    reps_of = [(rep + r) & (REPS - 1) for r in range(REPS)]
+
+    def target(shift, member):
+        return (chip + shift) * CORES + cores_of[member[0]], reps_of[member[1]]
+
+    def signal(semaphore, shift, member):
+        pl.semaphore_signal(
+            semaphore, inc=1, device_id=target(shift, member), device_id_type=MESH
+        )
+
+    def count_of(flags):
+        return sum(flags[n].astype(jnp.int32) for n in shifts)
+
+    right = (state, reps_of[1])
+    left = (state, reps_of[3])
+    width = held // CHUNKS
+
+    def piece(ref, chunk):
+        return ref.at[:, pl.ds(chunk * width, width)]
+
+    def bulk(source, owner, chunk, target, send_sem, recv_sem):
+        return pltpu.make_async_remote_copy(
+            src_ref=piece(source, chunk),
+            dst_ref=piece(all_ref.at[owner], chunk),
+            send_sem=send_sem.at[chunk],
+            recv_sem=recv_sem.at[chunk],
+            device_id=target,
+            device_id_type=MESH,
+        )
+
+    half = CHUNKS // 2
+    to_right = [bulk(ens_ref, rep, c, right, send_right, recv_left) for c in range(CHUNKS)]
+    to_left = [bulk(ens_ref, rep, c, left, send_left, recv_right) for c in range(CHUNKS)]
+    barrier = pltpu.get_barrier_semaphore()
+
+    def straight(n):
+        other = depth + n
+        apart = (chip + n) ^ chip
+        low = (depth > 0) & (other > 0) & (depth < DEPTH // 2) & (other < DEPTH // 2)
+        return valid[n] & (((apart & (DEPTH // 2)) != 0) | (low & ((apart & WINDOW) != 0)))
+
+    crosses = {n: straight(n) for n in shifts}
+    greetings = (
+        len(peers)
+        + (1 - core)
+        + count_of(earlier)
+        + (len(members) - 1) * count_of({n: earlier[n] & crosses[n] for n in shifts})
+    )
+    for member in peers:
+        signal(barrier, 0, member)
+
+    @pl.when(core == 1)
+    def _():
+        signal(barrier, 0, pair)
+
     load = pltpu.make_async_copy(ens_ref, fetch_ref, local_sem)
     load.start()
     smalls = [
@@ -64,76 +134,6 @@
     ]
     for small in smalls:
         small.start()
-
-    depth = chip & (DEPTH - 1)
-    shifts = list(range(1, WINDOW + 1)) + list(range(-1, -WINDOW - 1, -1))
-    valid = {n: (chip + n >= 0) & (chip + n < chips) for n in shifts}
-
-    def key(place):
-        return place + jnp.where((place >> 2) == 2, DEPTH, 0)
-
-    ahead = {n: key((depth + n) & (DEPTH - 1)) > key(depth) for n in shifts}
-    later = {n: valid[n] & ahead[n] for n in shifts}
-    earlier = {n: valid[n] & jnp.logical_not(ahead[n]) for n in shifts}
-    members = [(c, r) for c in range(CORES) for r in range(REPS)]
-    beside = members[1:]
-    peers = members[1:REPS]
-    pair = members[REPS]
-    cores_of = [core, 1 - core]
-    reps_of = [(rep + r) & (REPS - 1) for r in range(REPS)]
-
-    def target(shift, member):
-        return (chip + shift) * CORES + cores_of[member[0]], reps_of[member[1]]
-
-    def signal(semaphore, shift, member):
-        pl.semaphore_signal(
-            semaphore, inc=1, device_id=target(shift, member), device_id_type=MESH
-        )
-
-    def count_of(flags):
-        return sum(flags[n].astype(jnp.int32) for n in shifts)
-
-    right = (state, reps_of[1])
-    left = (state, reps_of[3])
-    width = held // CHUNKS
-
-    def piece(ref, chunk):
-        return ref.at[:, pl.ds(chunk * width, width)]
-
-    def bulk(source, owner, chunk, target, send_sem, recv_sem):
-        return pltpu.make_async_remote_copy(
-            src_ref=piece(source, chunk),
-            dst_ref=piece(all_ref.at[owner], chunk),
-            send_sem=send_sem.at[chunk],
-            recv_sem=recv_sem.at[chunk],
-            device_id=target,
-            device_id_type=MESH,
-        )
-
-    half = CHUNKS // 2
-    to_right = [bulk(ens_ref, rep, c, right, send_right, recv_left) for c in range(CHUNKS)]
-    to_left = [bulk(ens_ref, rep, c, left, send_left, recv_right) for c in range(CHUNKS)]
-    barrier = pltpu.get_barrier_semaphore()
-
-    def straight(n):
-        other = depth + n
-        apart = (chip + n) ^ chip
-        low = (depth > 0) & (other > 0) & (depth < DEPTH // 2) & (other < DEPTH // 2)
-        return valid[n] & (((apart & (DEPTH // 2)) != 0) | (low & ((apart & WINDOW) != 0)))
-
-    crosses = {n: straight(n) for n in shifts}
-    greetings = (
-        len(peers)
-        + (1 - core)
-        + count_of(earlier)
-        + (len(members) - 1) * count_of({n: earlier[n] & crosses[n] for n in shifts})
-    )
-    for member in peers:
-        signal(barrier, 0, member)
-
-    @pl.when(core == 1)
-    def _():
-        signal(barrier, 0, pair)
 
     for n in shifts:
 

time: 22 us -> 22.6 us (1.027)
  the two profiles are of different devices: /device:TPU:1 before, /device:TPU:7 now
where the time goes in v10:
time: 22.6 us; the launch traced here: 22.4 us
  Pallas kernels  21.8 us (96%)
  between operations  0.57 us (3%)
    pallas_call x1, Pallas kernels, gather(): pl.pallas_call(functools.partial(gather_kernel, mesh.shape['state'] // CO...  18 us
    pallas_call x1, Pallas kernels, solve(): pl.pallas_call(functools.partial(solve_kernel, windowed, held), out_shape...  3.78 us

profile of v10, /device:TPU:7, one launch (start us, length us, event | category | flops | bytes accessed | tf_op | source)
XLA Modules:
  0.0 22.4 jit_solution(1716722660127334633)
XLA Ops:
  0.0 18.0 %gather.9 = (f32[72,1,128]{2,1,0:T(1,128)S(1)}, f32[4,16,4096]{2,1,0:T(8,128)S(1)}, f32[8,128]{1,0:T(8,128)S(1)}, s32[1,1]{1,0:T(1,128)}) custom-call(s32[48]{0:T(128)} %loc_any.1, f32[48]{0:T(128)} %val_any.1, f32[48]{0:T(128)} %err_any.1, f32[16,4096]{1,0:T(8,128)} %ens_ref.1), custom_call_target="tpu_custom_call" | custom-call | tf_op jit(solution)/shard_map/gather/pallas_call | solution.py:363
  18.6 3.8 %conditional.1 = (f32[16,4096]{1,0:T(8,128)}) conditional(s32[]{:T(128)} %bitcast.5, (f32[8,128]{1,0:T(8,128)S(1)}, f32[72,1,128]{2,1,0:T(1,128)S(1)}, f32[4,16,4096]{2,1,0:T(8,128)S(1)}) %tuple.11, (s32[48]{0:T(128)}, f32[16,4096]{1,0:T(8,128)}, f32[8,128]{1,0:T(8,128)S(1)}, f32[4,16,4096]{2,1,0:T(8,128)S(1)}) %tuple.12), branch_computations={%region_0.0_spmd, %region_1.2_spmd} | conditional | flops 30025 | bytes 1545686 | solution.py:552
  18.6 3.8 %solve.2 = f32[16,4096]{1,0:T(8,128)} custom-call(f32[8,128]{1,0:T(8,128)S(1)} %get-tuple-element.22.table_ref, f32[72,1,128]{2,1,0:T(1,128)S(1)} %get-tuple-element.23.rows_ref, f32[4,16,4096]{2,1,0:T(8,128)S(1)} %get-tuple-element.24.all_ref), custom_call_target="tpu_custom_call" | custom-call | tf_op jit(solution)/shard_map/cond/branch_0_fun/solve/pallas_call | solution.py:509

commit v11 on v10

--- a/solution.py
+++ b/solution.py
@@ -469,7 +469,7 @@
         return carry
 
     lax.fori_loop(0, total, assimilate, 0)
-    group = 4
+    group = 8
 
     def apply(g, carry):
         spans = [

time: 22.6 us -> 22.2 us (0.982)
  the two profiles are of different devices: /device:TPU:7 before, /device:TPU:1 now
where the time goes in v11:
time: 22.2 us; the launch traced here: 22 us
  Pallas kernels  21.4 us (96%)
  between operations  0.57 us (3%)
    pallas_call x1, Pallas kernels, gather(): pl.pallas_call(functools.partial(gather_kernel, mesh.shape['state'] // CO...  18.6 us
    pallas_call x1, Pallas kernels, solve(): pl.pallas_call(functools.partial(solve_kernel, windowed, held), out_shape...  2.81 us

profile of v11, /device:TPU:1, one launch (start us, length us, event | category | flops | bytes accessed | tf_op | source)
XLA Modules:
  0.0 22.0 jit_solution(10576077342759107325)
XLA Ops:
  0.0 18.6 %gather.9 = (f32[72,1,128]{2,1,0:T(1,128)S(1)}, f32[4,16,4096]{2,1,0:T(8,128)S(1)}, f32[8,128]{1,0:T(8,128)S(1)}, s32[1,1]{1,0:T(1,128)}) custom-call(s32[48]{0:T(128)} %loc_any.1, f32[48]{0:T(128)} %val_any.1, f32[48]{0:T(128)} %err_any.1, f32[16,4096]{1,0:T(8,128)} %ens_ref.1), custom_call_target="tpu_custom_call" | custom-call | tf_op jit(solution)/shard_map/gather/pallas_call | solution.py:363
  19.2 2.8 %conditional.1 = (f32[16,4096]{1,0:T(8,128)}) conditional(s32[]{:T(128)} %bitcast.5, (f32[8,128]{1,0:T(8,128)S(1)}, f32[72,1,128]{2,1,0:T(1,128)S(1)}, f32[4,16,4096]{2,1,0:T(8,128)S(1)}) %tuple.11, (s32[48]{0:T(128)}, f32[16,4096]{1,0:T(8,128)}, f32[8,128]{1,0:T(8,128)S(1)}, f32[4,16,4096]{2,1,0:T(8,128)S(1)}) %tuple.12), branch_computations={%region_0.0_spmd, %region_1.2_spmd} | conditional | flops 30025 | bytes 1545686 | solution.py:552
  19.2 2.8 %solve.2 = f32[16,4096]{1,0:T(8,128)} custom-call(f32[8,128]{1,0:T(8,128)S(1)} %get-tuple-element.22.table_ref, f32[72,1,128]{2,1,0:T(1,128)S(1)} %get-tuple-element.23.rows_ref, f32[4,16,4096]{2,1,0:T(8,128)S(1)} %get-tuple-element.24.all_ref), custom_call_target="tpu_custom_call" | custom-call | tf_op jit(solution)/shard_map/cond/branch_0_fun/solve/pallas_call | solution.py:509
